TPU v7x, 256 devices: a whole 4x4x8 slice. The times are simulated.
256 devices in a mesh: freq: 8 (over z), dom: 32 (over y, x, core).
Axes of the slice: x: 4, y: 4, z: 8, core: 2. Of those that a mesh axis runs over, the one named last changes fastest.
Arguments:
- angular: float32 [16], P('freq'), may hold values from 0.5 to 4
- stiffness: float32 [32, 36, 1024], P('dom'), as said below
- mass_matrix: float32 [32, 36, 1024], P('dom'), as said below
- conductivity: float32 [32, 1024], P('dom'), may hold values from 0.3 to 3
- element_edges: int32 [32, 6, 1024], P('dom'), may hold values from 0 to 1279
- live_slots: int32 [32, 1024], P('dom'), may hold values from 0 to 1, as said below
- adjoint_source: float32 [16, 2, 32, 1280], P('freq', None, 'dom'), may hold values from -6 to 6
- forward_field: float32 [16, 2, 32, 1280], P('freq', None, 'dom'), may hold values from -6 to 6
- neighbour_map: int32 [32, 256], P('dom'), may hold values from 0 to 255, each once within a row
Outputs:
- gradient: float32 [32, 1024], P('dom')
- updated_conductivity: float32 [32, 1024], P('dom')
Inputs may be any that keep to these rules, and one draw needn't show every extreme that they name: `live_slots`: in each partition the live slots come first; at least half of the 1024 slots are live, and some partition has all slots live. `neighbour_map`: each row is a permutation of the rim slots; row 0 is not used. `stiffness`: each element matrix is symmetric with a strictly dominant positive diagonal. `mass_matrix`: each element matrix is symmetric with a strictly dominant positive diagonal.
All inputs are finite; a program needn't handle non-finite values.
Results may differ from a plain program's by a relative error of at most 0.0003.
Values sent between devices are 32-bit elements; how exact they have to be, the bound alone decides.
A program may use at most 64 MiB of HBM per device.

v0:
```python
import jax
import jax.numpy as jnp
from jax import lax
from jax.sharding import PartitionSpec as P

ITERS = 3


highest = lax.Precision.HIGHEST


def passed_along(block, axis, distance):
    devices = range(lax.axis_size(axis))
    route = [(i - distance, i) for i in devices if i - distance in devices]
    return lax.ppermute(block, axis, route)


def element_blocks(angular, stiffness, mass_matrix, conductivity, live_slots):
    weights = live_slots.astype(jnp.float32)
    shifted = angular[:, None, None] * (conductivity * weights)[None, None, :]
    return stiffness[None] * weights[None, None, :] + shifted * mass_matrix[None]


def edge_table(edge_row, edge_count):
    return (edge_row[:, None] == jnp.arange(edge_count, dtype=jnp.int32)[None, :]).astype(
        jnp.bfloat16
    )


def pick_one(vector_in, table):
    return jnp.einsum(
        "gpe,ke->gpk",
        vector_in,
        table.astype(jnp.float32),
        precision=highest,
        preferred_element_type=jnp.float32,
    )


def local_apply(blocks, vector_in, edge_ids):
    edge_count = vector_in.shape[-1]
    tables = [edge_table(edge_ids[j], edge_count) for j in range(6)]
    picked = [pick_one(vector_in, tables[j]) for j in range(6)]
    total = jnp.zeros_like(vector_in)
    for i in range(6):
        running = blocks[:, None, 6 * i, :] * picked[0]
        for j in range(1, 6):
            running = running + blocks[:, None, 6 * i + j, :] * picked[j]
        total = total + jnp.einsum(
            "gpk,ke->gpe",
            running,
            tables[i].astype(jnp.float32),
            precision=highest,
            preferred_element_type=jnp.float32,
        )
    return total


def element_gradient(angular, mass_matrix, live_slots, adjoint, forward_local, edge_ids):
    edge_count = adjoint.shape[-1]
    tables = [edge_table(edge_ids[j], edge_count) for j in range(6)]
    forward_picked = [pick_one(forward_local, tables[j]) for j in range(6)]
    inner_terms = jnp.zeros((adjoint.shape[0], adjoint.shape[1], edge_ids.shape[1]), jnp.float32)
    for i in range(6):
        running = mass_matrix[None, None, 6 * i, :] * forward_picked[0]
        for j in range(1, 6):
            running = running + mass_matrix[None, None, 6 * i + j, :] * forward_picked[j]
        inner_terms = inner_terms + pick_one(adjoint, tables[i]) * running
    inner_terms = jnp.sum(inner_terms, axis=1)
    return -jnp.sum(angular[:, None] * inner_terms, axis=0) * live_slots.astype(jnp.float32)


def join_rims(vectors, permuter):
    rim = permuter.shape[0]
    edge_count = vectors.shape[-1]
    lower_rim = vectors[..., :rim]
    upper_rim = vectors[..., edge_count - rim :]
    arranged = jnp.einsum(
        "gpi,ij->gpj", lower_rim, permuter, precision=highest, preferred_element_type=jnp.float32
    )
    from_above = passed_along(arranged, "dom", -1)
    from_prior = passed_along(upper_rim, "dom", 1)
    from_below = jnp.einsum(
        "gpj,ij->gpi", from_prior, permuter, precision=highest, preferred_element_type=jnp.float32
    )
    middle = vectors[..., rim : edge_count - rim]
    return jnp.concatenate([lower_rim + from_below, middle, upper_rim + from_above], axis=-1)


def local(
    angular,
    stiffness,
    mass_matrix,
    conductivity,
    element_edges,
    live_slots,
    adjoint_source,
    forward_field,
    neighbour_map,
):
    order = neighbour_map[0]
    edge_ids = element_edges[0]
    sources = adjoint_source[:, :, 0, :]
    forward_local = forward_field[:, :, 0, :]
    edge_count = sources.shape[-1]
    rim = order.shape[0]
    permuter = (order[:, None] == jnp.arange(rim, dtype=jnp.int32)[None, :]).astype(jnp.float32)
    blocks = element_blocks(angular, stiffness[0], mass_matrix[0], conductivity[0], live_slots[0])
    owned = jnp.where(
        (jnp.arange(edge_count) < rim) & (lax.axis_index("dom") > 0), 0.0, 1.0
    ).astype(jnp.float32)

    def local_inner(first, second):
        return jnp.sum(first * second * owned, axis=-1)

    def residual_norm(vector_now):
        return lax.psum(local_inner(vector_now, vector_now), "dom")

    rhs = join_rims(sources, permuter)
    adjoint = jnp.zeros_like(rhs)
    residual = rhs
    direction = rhs
    norm_now = residual_norm(residual)
    for step in range(ITERS):
        image = join_rims(local_apply(blocks, direction, edge_ids), permuter)
        curve = lax.psum(local_inner(direction, image), "dom")
        alpha = (norm_now / curve)[..., None]
        adjoint = adjoint + alpha * direction
        residual = residual - alpha * image
        norm_next = residual_norm(residual)
        direction = residual + (norm_next / norm_now)[..., None] * direction
        norm_now = norm_next
    term = element_gradient(
        angular, mass_matrix[0], live_slots[0], adjoint, forward_local, edge_ids
    )
    gradient = lax.psum(term, "freq")
    updated = conductivity[0] * jnp.exp(-0.5 * jnp.tanh(gradient))
    return (gradient[None], updated[None])


def solution(mesh):
    return jax.shard_map(
        local,
        mesh=mesh,
        in_specs=(
            P("freq"),
            P("dom", None, None),
            P("dom", None, None),
            P("dom", None),
            P("dom", None, None),
            P("dom", None),
            P("freq", None, "dom", None),
            P("freq", None, "dom", None),
            P("dom", None),
        ),
        out_specs=(P("dom", None), P("dom", None)),
        check_vma=False,
    )
```

profile of v0, /device:TPU:0, one launch (start us, length us, event | category | flops | bytes accessed | tf_op | source)
XLA Modules:
  0.0 482.5 jit_solution(17898827815151689793)
XLA Ops:
  2.3 1.3 collective-permute-start.1
  6.4 3.0 collective-permute-start
  10.6 2.5 fusion.15
  13.1 2.5 fusion.32
  15.6 2.5 fusion.49
  18.2 2.5 fusion.66
  20.7 2.5 fusion.83
  23.2 2.5 fusion.100
  25.7 2.1 fusion.13
  27.8 1.9 fusion.186
  29.7 1.9 fusion.177
  31.6 1.9 fusion.168
  33.5 1.9 fusion.159
  35.4 1.9 fusion.150
  37.5 1.3 collective-permute-start.3
  38.9 1.7 collective-permute-done.3
  40.6 4.2 collective-permute-start.2
  46.1 65.9 %all-reduce = (f32[2,2]{1,0:T(2,128)S(1)}, f32[2,2]{1,0:T(2,128)S(1)}) all-reduce(f32[2,2]{1,0:T(2,128)S(1)} %get-tuple-element.3, f32[2,2]{1,0:T(2,128)S(1)} %get-tuple-element.2), channel_id=1, replica_groups=mesh['freq'=8,'dom'=32] {'dom'}, use_global_device_ids=true, to_apply=%region_1.2 | all-reduce | flops 8 | bytes 64 | tf_op jit(solution)/shard_map/psum | solution.py:117
  112.2 63.1 %psum.51 = f32[2,2]{1,0:T(2,128)S(1)} all-reduce(f32[2,2]{1,0:T(2,128)S(1)} %get-tuple-element.6), channel_id=1, replica_groups=mesh['freq'=8,'dom'=32] {'dom'}, use_global_device_ids=true, to_apply=%region_5.6 | all-reduce | flops 4 | bytes 32 | tf_op jit(solution)/shard_map/psum | solution.py:117
  175.4 2.5 fusion.11
  177.9 2.5 fusion.28
  180.4 2.5 fusion.45
  182.9 2.5 fusion.62
  185.5 2.5 fusion.79
  188.0 2.5 fusion.96
  190.5 2.1 fusion.9
  192.6 1.9 fusion.189
  194.5 1.9 fusion.180
  196.4 1.9 fusion.171
  198.2 1.9 fusion.162
  200.1 1.9 fusion.153
  202.3 1.3 collective-permute-start.5
  203.6 1.7 collective-permute-done.5
  205.4 3.6 collective-permute-start.4
  209.0 2.5 fusion.1
  211.9 2.5 fusion.20
  214.4 62.7 %psum.52 = f32[2,2]{1,0:T(2,128)S(1)} all-reduce(f32[2,2]{1,0:T(2,128)S(1)} %multiply_reduce_fusion.1), channel_id=1, replica_groups=mesh['freq'=8,'dom'=32] {'dom'}, use_global_device_ids=true, to_apply=%region_7.8 | all-reduce | flops 4 | bytes 32 | tf_op jit(solution)/shard_map/psum | solution.py:126
  277.3 2.5 fusion.37
  279.8 63.1 %psum.53 = f32[2,2]{1,0:T(2,128)S(1)} all-reduce(f32[2,2]{1,0:T(2,128)S(1)} %multiply_reduce_fusion), channel_id=1, replica_groups=mesh['freq'=8,'dom'=32] {'dom'}, use_global_device_ids=true, to_apply=%region_9.10 | all-reduce | flops 4 | bytes 32 | tf_op jit(solution)/shard_map/psum | solution.py:117
  342.9 2.5 fusion.24
  345.4 2.5 fusion.41
  348.0 2.5 fusion.58
  350.5 2.5 fusion.7
  353.0 2.5 fusion.75
  355.5 2.5 fusion.92
  358.1 2.1 fusion.5
  360.1 1.9 fusion.192
  362.0 1.9 fusion.183
  363.9 1.9 fusion.174
  365.8 1.9 fusion.165
  367.7 1.9 fusion.156
  369.9 1.3 collective-permute-start.7
  371.2 2.5 fusion.54
  373.7 3.0 collective-permute-start.6
  376.7 2.5 fusion.71
  379.6 2.5 fusion.88
  382.1 64.0 %psum.54 = f32[2,2]{1,0:T(2,128)S(1)} all-reduce(f32[2,2]{1,0:T(2,128)S(1)} %fusion.259), channel_id=1, replica_groups=mesh['freq'=8,'dom'=32] {'dom'}, use_global_device_ids=true, to_apply=%region_11.12 | all-reduce | flops 4 | bytes 32 | tf_op jit(solution)/shard_map/psum | solution.py:126
  446.2 2.5 fusion.225
  448.7 2.5 fusion.222
  451.3 2.5 fusion.216
  453.8 2.5 fusion.210
  456.3 2.5 fusion.204
  458.9 2.5 fusion.228
  461.5 20.0 %psum.55 = f32[1024]{0:T(1024)S(1)} all-reduce(f32[1024]{0:T(1024)S(1)} %negate_multiply_fusion), channel_id=1, replica_groups=mesh['freq'=8,'dom'=32] {'freq'}, use_global_device_ids=true, to_apply=%region_14.15 | all-reduce | flops 1024 | bytes 8192 | tf_op jit(solution)/shard_map/psum | solution.py:136
  (66 shorter events, 9.7 us)
Async XLA Ops:
  0.6 4.7 copy-start.2
  0.6 4.8 copy-start
  2.3 4.0 collective-permute-start.1
  5.4 0.7 copy-start.4
  6.3 3.1 copy-start.1
  6.3 3.9 copy-start.6
  6.4 3.8 collective-permute-start
  37.5 3.1 collective-permute-start.3
  40.6 5.1 %collective-permute-start.2 = (f32[2,2,256]{2,1,0:T(2,128)S(1)}, f32[2,2,256]{2,1,0:T(2,128)S(1)}, u32[]{:S(2)}, u32[]{:S(2)}) collective-permute-start(f32[2,2,256]{2,1,0:T(2,128)S(1)} %get-tuple-element.90), channel_id=1, source_target_pairs={{0,1},{1,2},{2,3},{3,4},{4,5},{5,6},{6,7},{7,8},{8,9},{9,10},{10,1... | collective-permute-start | bytes 12296 | tf_op jit(solution)/shard_map/ppermute | solution.py:15
  200.1 8.9 %copy-start.5 = (f32[2,2,1,1280]{3,2,1,0:T(1,128)S(1)}, f32[2,2,1,1280]{3,2,1,0:T(1,128)}, u32[]{:S(2)}) copy-start(f32[2,2,1,1280]{3,2,1,0:T(1,128)} %param.16) | copy-start | bytes 61444
  202.3 3.1 collective-permute-start.5
  205.4 6.1 %collective-permute-start.4 = (f32[2,2,256]{2,1,0:T(2,128)S(1)}, f32[2,2,256]{2,1,0:T(2,128)S(1)}, u32[]{:S(2)}, u32[]{:S(2)}) collective-permute-start(f32[2,2,256]{2,1,0:T(2,128)S(1)} %get-tuple-element.88), channel_id=1, source_target_pairs={{0,1},{1,2},{2,3},{3,4},{4,5},{5,6},{6,7},{7,8},{8,9},{9,10},{10,1... | collective-permute-start | bytes 12296 | tf_op jit(solution)/shard_map/ppermute | solution.py:15
  369.9 3.8 collective-permute-start.7
  373.7 5.5 %collective-permute-start.6 = (f32[2,2,256]{2,1,0:T(2,128)S(1)}, f32[2,2,256]{2,1,0:T(2,128)S(1)}, u32[]{:S(2)}, u32[]{:S(2)}) collective-permute-start(f32[2,2,256]{2,1,0:T(2,128)S(1)} %get-tuple-element.86), channel_id=1, source_target_pairs={{0,1},{1,2},{2,3},{3,4},{4,5},{5,6},{6,7},{7,8},{8,9},{9,10},{10,1... | collective-permute-start | bytes 12296 | tf_op jit(solution)/shard_map/ppermute | solution.py:15
  481.5 0.6 copy-start.3
where the time goes:
time: 492 us; the launch traced here: 483 us
  blocking collectives  339 us (69%)
  matrix products  113 us (23%)
  starting transfers between devices  19.1 us (4%)
  waiting for transfers between devices  5.06 us (1%)
    psum x3, blocking collectives, residual_norm(): return lax.psum(local_inner(vector_now, vector_now), 'dom')  192 us
    psum x2, blocking collectives, local(): curve = lax.psum(local_inner(direction, image), 'dom')  127 us
    dot_general x30, matrix products, pick_one(): jnp.einsum('gpe,ke->gpk', vector_in, table.astype(jnp.float32), precision...  75.4 us
    dot_general x18, matrix products, local_apply(): jnp.einsum('gpk,ke->gpe', running, tables[i].astype(jnp.float32), precisi...  34.6 us
    psum x1, blocking collectives, local(): gradient = lax.psum(term, 'freq')  20 us
    ppermute x8, starting transfers between devices, passed_along(): return lax.ppermute(block, axis, route)  19.1 us
  transfers between devices with their start and end apart: 8, of which 4 were waited for; matrix products, arithmetic and copies ran while one was open for 2% of the time, Pallas kernels for 0%

commit v1 on v0

v1 whole, which is shorter than its diff:
```python
import jax
import jax.numpy as jnp
from jax import lax
from jax.experimental import pallas as pl
from jax.experimental.pallas import tpu as pltpu
from jax.sharding import PartitionSpec as P

MESH = pl.DeviceIdType.MESH
F32 = jnp.float32
BF16 = jnp.bfloat16
DOM = 32
FREQ = 8
RIM = 256
EDGES = 1280
HALF = 512
CHUNKS = EDGES // 128
WIDE = EDGES // RIM
PARTS = 2


def rows_iota(shape):
    return lax.broadcasted_iota(jnp.int32, shape, 0)


def lanes_iota(shape):
    return lax.broadcasted_iota(jnp.int32, shape, 1)


def lane_pick(table, lane):
    return jnp.take_along_axis(table, lane, axis=1, mode="promise_in_bounds")


def two_halves(row):
    first = jnp.broadcast_to(row[:, :HALF], (8, HALF))
    second = jnp.broadcast_to(row[:, HALF:], (8, HALF))
    return jnp.where(rows_iota((8, HALF)) < 4, first, second)


def eight_rows(row):
    out = jnp.broadcast_to(row[:, :128], (8, 128))
    for r in range(1, 8):
        piece = jnp.broadcast_to(row[:, 128 * r : 128 * (r + 1)], (8, 128))
        out = jnp.where(rows_iota((8, 128)) == r, piece, out)
    return out


def field_rows(ref):
    out = jnp.broadcast_to(ref[0, 0], (8, EDGES))
    kind = rows_iota((8, EDGES)) % 4
    for v in range(1, 4):
        out = jnp.where(kind == v, jnp.broadcast_to(ref[v // 2, v % 2], (8, EDGES)), out)
    return out


def permuted(rim, order):
    out = []
    for q in range(2):
        index = order[:, 128 * q : 128 * (q + 1)]
        lane = index & 127
        low = lane_pick(rim[:, :128], lane)
        high = lane_pick(rim[:, 128:], lane)
        out.append(jnp.where(index < 128, low, high))
    return jnp.concatenate(out, axis=1)


def edge_dot(a, b, own=None):
    total = a[:, 256:384] * b[:, 256:384]
    for c in range(3, CHUNKS):
        total = total + a[:, 128 * c : 128 * (c + 1)] * b[:, 128 * c : 128 * (c + 1)]
    rim = a[:, :128] * b[:, :128] + a[:, 128:256] * b[:, 128:256]
    return total + (rim if own is None else own * rim)


def kernel(
    angular,
    stiffness_hbm,
    mass_hbm,
    conductivity_hbm,
    edges_hbm,
    live_hbm,
    source_hbm,
    forward_hbm,
    order_hbm,
    gradient_ref,
    updated_ref,
    stiffness,
    mass,
    conductivity,
    edges,
    live,
    source,
    forward,
    order,
    ids,
    masks,
    onehot,
    blocks,
    picked,
    weight,
    values,
    down_out,
    up_out,
    down_in,
    up_in,
    sums,
    terms,
    load_sem,
    down_send,
    down_recv,
    up_send,
    up_recv,
    sum_send,
    sum_recv,
    term_send,
    term_recv,
):
    me = lax.axis_index("dom")
    my_freq = lax.axis_index("freq")
    below = lax.rem(me + DOM - 1, DOM)
    above = lax.rem(me + 1, DOM)

    loads = [
        pltpu.make_async_copy(src, dst, load_sem.at[n])
        for n, (src, dst) in enumerate(
            [
                (source_hbm, source),
                (order_hbm, order),
                (edges_hbm.at[0], edges),
                (forward_hbm, forward),
                (conductivity_hbm, conductivity),
                (live_hbm, live),
                (stiffness_hbm.at[0], stiffness),
                (mass_hbm.at[0], mass),
            ]
        )
    ]
    for load in loads:
        load.start()

    barrier = pltpu.get_barrier_semaphore()
    for k in range(1, DOM):
        peer = lax.rem(me + k, DOM)
        pl.semaphore_signal(barrier, inc=1, device_id=(my_freq, peer), device_id_type=MESH)
    for k in range(1, FREQ):
        peer = lax.rem(my_freq + k, FREQ)
        pl.semaphore_signal(barrier, inc=1, device_id=(peer, me), device_id_type=MESH)

    loads[0].wait()
    loads[1].wait()
    order_rows = jnp.broadcast_to(order[...], (8, RIM))
    match = jnp.where(rows_iota((RIM, RIM)) == jnp.broadcast_to(order[...], (RIM, RIM)), 1.0, 0.0)
    inverse = lax.dot_general(
        lanes_iota((8, RIM)).astype(F32).astype(BF16),
        match.astype(BF16),
        (((1,), (1,)), ((), ())),
        preferred_element_type=F32,
    ).astype(jnp.int32)
    sources = field_rows(source)

    def send_rims(k, field):
        down_out[k] = permuted(field[:, :RIM], inverse)
        up_out[k] = field[:, EDGES - RIM :]
        copies = (
            pltpu.make_async_remote_copy(
                src_ref=down_out.at[k],
                dst_ref=down_in.at[k],
                send_sem=down_send.at[k],
                recv_sem=down_recv.at[k],
                device_id=(my_freq, below),
                device_id_type=MESH,
            ),
            pltpu.make_async_remote_copy(
                src_ref=up_out.at[k],
                dst_ref=up_in.at[k],
                send_sem=up_send.at[k],
                recv_sem=up_recv.at[k],
                device_id=(my_freq, above),
                device_id_type=MESH,
            ),
        )
        for copy in copies:
            copy.start()
        return copies

    def join_rims(k, copies, field):
        for copy in copies:
            copy.wait()
        zero = jnp.zeros((8, RIM), F32)
        from_below = jnp.where(me > 0, permuted(up_in[k], order_rows), zero)
        from_above = jnp.where(me < DOM - 1, down_in[k], zero)
        return jnp.concatenate(
            [
                field[:, :RIM] + from_below,
                field[:, RIM : EDGES - RIM],
                field[:, EDGES - RIM :] + from_above,
            ],
            axis=1,
        )

    pl.semaphore_wait(barrier, DOM - 1 + FREQ - 1)
    rim_copies = send_rims(0, sources)

    loads[2].wait()
    for i in range(6):
        row = edges[i : i + 1, :]
        ids[i] = two_halves(row)
        wide = ids[i] >> 8
        for c in range(WIDE):
            hit = jnp.where(wide == c, 1.0, 0.0)
            masks[c, :, HALF * i : HALF * (i + 1)] = jnp.concatenate([hit] * PARTS, axis=0).astype(BF16)
        for h in range(2):
            low = jnp.broadcast_to(row[:, HALF * h : HALF * (h + 1)] & (RIM - 1), (RIM, HALF))
            hit = jnp.where(rows_iota((RIM, HALF)) == low, 1.0, 0.0)
            onehot[RIM * h : RIM * (h + 1), HALF * i : HALF * (i + 1)] = hit.astype(BF16)

    def pick(field):
        def one(i, carry):
            for q in range(4):
                index = ids[i, :, 128 * q : 128 * (q + 1)]
                lane = index & 127
                found = [lane_pick(field[:, 128 * c : 128 * (c + 1)], lane) for c in range(CHUNKS)]
                bit = 7
                while len(found) > 1:
                    odd = (index & (1 << bit)) != 0
                    merged = [
                        jnp.where(odd, found[n + 1], found[n]) for n in range(0, len(found) - 1, 2)
                    ]
                    if len(found) % 2:
                        merged.append(found[-1])
                    found = merged
                    bit += 1
                picked[i, :, 128 * q : 128 * (q + 1)] = found[0]
            return carry

        for i in range(6):
            one(i, 0)

    loads[3].wait()
    pick(field_rows(forward))
    loads[4].wait()
    loads[5].wait()
    alive = two_halves(live[...]).astype(F32)
    cond_rows = two_halves(conductivity[...])
    freq_of = rows_iota((8, HALF)) % 4 < 2
    omega = jnp.where(freq_of, angular[0], angular[1])
    shift = omega * (cond_rows * alive)
    sign = -(omega * alive)
    cond_eight = eight_rows(conductivity[...])
    loads[6].wait()
    loads[7].wait()
    for i in range(6):
        running = None
        for j in range(6):
            n = 6 * i + j
            mass_rows = two_halves(mass[n : n + 1, :])
            blocks[n] = two_halves(stiffness[n : n + 1, :]) * alive + shift * mass_rows
            product = mass_rows * picked[j]
            running = product if running is None else running + product
        weight[i] = sign * running

    def apply(field):
        pick(field)
        term = weight[0] * picked[0]
        for i in range(1, 6):
            term = term + weight[i] * picked[i]
        for i in range(6):
            running = blocks[6 * i] * picked[0]
            for j in range(1, 6):
                running = running + blocks[6 * i + j] * picked[j]
            pieces = []
            rest = running
            for _ in range(PARTS - 1):
                head = rest.astype(BF16).astype(F32)
                pieces.append(head)
                rest = rest - head
            pieces.append(rest)
            stacked = jnp.concatenate(pieces, axis=0).astype(BF16)
            for c in range(WIDE):
                values[8 * PARTS * c : 8 * PARTS * (c + 1), HALF * i : HALF * (i + 1)] = (
                    stacked * masks[c, :, HALF * i : HALF * (i + 1)]
                )
        out = lax.dot_general(
            values[...], onehot[...], (((1,), (1,)), ((), ())), preferred_element_type=F32
        )
        pieces = []
        for c in range(WIDE):
            halves = out[8 * PARTS * c : 8 * PARTS * c + 8]
            for s in range(1, PARTS):
                halves = halves + out[8 * PARTS * c + 8 * s : 8 * PARTS * c + 8 * s + 8]
            mixed = jnp.where(rows_iota((8, RIM)) < 4, halves[:, :RIM], halves[:, RIM:])
            pieces.append(mixed + pltpu.roll(mixed, 4, 0))
        return jnp.concatenate(pieces, axis=1), term

    lane = lanes_iota((8, 128))
    sub = rows_iota((8, 128))

    def send_sums(k, quantities):
        row = jnp.zeros((8, 128), F32)
        for n, quantity in enumerate(quantities):
            column = jnp.sum(quantity, axis=1, keepdims=True)
            row = row + jnp.where((lane == 4 * n + sub) & (sub < 4), column, 0.0)
        sums[k, me] = jnp.sum(row, axis=0, keepdims=True)
        copies = []
        for n in range(1, DOM):
            peer = lax.rem(me + n, DOM)
            copy = pltpu.make_async_remote_copy(
                src_ref=sums.at[k, me],
                dst_ref=sums.at[k, me],
                send_sem=sum_send.at[k],
                recv_sem=sum_recv.at[k],
                device_id=(my_freq, peer),
                device_id_type=MESH,
            )
            copy.start()
            copies.append(copy)

    def take_sums(k, count):
        rest = sums.at[k, pl.ds(0, DOM - 1)]
        pltpu.make_async_copy(rest, rest, sum_recv.at[k]).wait()
        total = jnp.broadcast_to(jnp.sum(sums[k], axis=0), (8, 128))
        return [
            jnp.sum(jnp.where(lane == 4 * n + sub % 4, total, 0.0), axis=1, keepdims=True)
            for n in range(count)
        ]

    own = jnp.where(me > 0, 0.0, 1.0).astype(F32)

    base = join_rims(0, rim_copies, sources)
    image0, term0 = apply(base)
    send_sums(0, [edge_dot(base, base, own), edge_dot(base, image0)])
    rim_copies = send_rims(1, image0)
    first = join_rims(1, rim_copies, image0)
    image1, term1 = apply(first)
    rim_copies = send_rims(2, image1)

    norm0, curve0 = take_sums(0, 2)
    alpha0 = norm0 / curve0
    residual1 = base - alpha0 * first
    local1 = image0 - alpha0 * image1
    send_sums(
        1,
        [
            edge_dot(residual1, residual1, own),
            edge_dot(residual1, local1),
            edge_dot(residual1, image0) + edge_dot(base, local1),
        ],
    )
    second = join_rims(2, rim_copies, image1)
    image2, term2 = apply(second)

    norm1, self1, cross1 = take_sums(1, 3)
    beta0 = norm1 / norm0
    curve1 = self1 + beta0 * cross1 + (beta0 * beta0) * curve0
    alpha1 = norm1 / curve1
    direction1 = residual1 + beta0 * base
    along1 = local1 + beta0 * image0
    residual2 = residual1 - alpha1 * ((first - alpha0 * second) + beta0 * first)
    local2 = local1 - alpha1 * ((image1 - alpha0 * image2) + beta0 * image1)
    send_sums(
        2,
        [
            edge_dot(residual2, residual2, own),
            edge_dot(residual2, local2),
            edge_dot(residual2, along1) + edge_dot(direction1, local2),
        ],
    )
    near1 = term0 - alpha0 * term1
    toward1 = near1 + beta0 * term0
    near2 = near1 - alpha1 * ((term1 - alpha0 * term2) + beta0 * term1)
    so_far = alpha0 * term0 + alpha1 * toward1

    norm2, self2, cross2 = take_sums(2, 3)
    beta1 = norm2 / norm1
    curve2 = self2 + beta1 * cross2 + (beta1 * beta1) * curve1
    alpha2 = norm2 / curve2
    total = so_far + alpha2 * (near2 + beta1 * toward1)

    total = total + pltpu.roll(total, 1, 0)
    total = total + pltpu.roll(total, 2, 0)
    packed = jnp.zeros((8, 128), F32)
    for h in range(2):
        for q in range(4):
            piece = jnp.broadcast_to(total[4 * h + 3 : 4 * h + 4, 128 * q : 128 * (q + 1)], (8, 128))
            packed = jnp.where(sub == 4 * h + q, piece, packed)
    terms[my_freq] = packed
    for n in range(1, FREQ):
        peer = lax.rem(my_freq + n, FREQ)
        pltpu.make_async_remote_copy(
            src_ref=terms.at[my_freq],
            dst_ref=terms.at[my_freq],
            send_sem=term_send,
            recv_sem=term_recv,
            device_id=(peer, me),
            device_id_type=MESH,
        ).start()
    rest = terms.at[pl.ds(0, FREQ - 1)]
    pltpu.make_async_copy(rest, rest, term_recv).wait()
    gradient = terms[0]
    for n in range(1, FREQ):
        gradient = gradient + terms[n]
    updated = cond_eight * jnp.exp(-0.5 * jnp.tanh(gradient))
    for r in range(8):
        gradient_ref[:, 128 * r : 128 * (r + 1)] = gradient[r : r + 1]
        updated_ref[:, 128 * r : 128 * (r + 1)] = updated[r : r + 1]

    pltpu.make_async_copy(rest, rest, term_send).wait()
    for k in range(3):
        sent = sums.at[k, pl.ds(0, DOM - 1)]
        pltpu.make_async_copy(sent, sent, sum_send.at[k]).wait()


def local(*args):
    hbm = pl.BlockSpec(memory_space=pltpu.MemorySpace.HBM)
    dma = pltpu.SemaphoreType.DMA
    outs = [jax.ShapeDtypeStruct((1, 1024), F32)] * 2
    return pl.pallas_call(
        kernel,
        out_shape=outs,
        in_specs=[pl.BlockSpec(memory_space=pltpu.MemorySpace.SMEM)] + [hbm] * 8,
        out_specs=[pl.BlockSpec(memory_space=pltpu.MemorySpace.VMEM)] * 2,
        scratch_shapes=[
            pltpu.VMEM((36, 1024), F32),
            pltpu.VMEM((36, 1024), F32),
            pltpu.VMEM((1, 1024), F32),
            pltpu.VMEM((6, 1024), jnp.int32),
            pltpu.VMEM((1, 1024), jnp.int32),
            pltpu.VMEM((2, 2, 1, EDGES), F32),
            pltpu.VMEM((2, 2, 1, EDGES), F32),
            pltpu.VMEM((1, RIM), jnp.int32),
            pltpu.VMEM((6, 8, HALF), jnp.int32),
            pltpu.VMEM((WIDE, 8 * PARTS, 6 * HALF), BF16),
            pltpu.VMEM((2 * RIM, 6 * HALF), BF16),
            pltpu.VMEM((36, 8, HALF), F32),
            pltpu.VMEM((6, 8, HALF), F32),
            pltpu.VMEM((6, 8, HALF), F32),
            pltpu.VMEM((8 * PARTS * WIDE, 6 * HALF), BF16),
            pltpu.VMEM((3, 8, RIM), F32),
            pltpu.VMEM((3, 8, RIM), F32),
            pltpu.VMEM((3, 8, RIM), F32),
            pltpu.VMEM((3, 8, RIM), F32),
            pltpu.VMEM((3, DOM, 1, 128), F32),
            pltpu.VMEM((FREQ, 8, 128), F32),
            dma((8,)),
            dma((3,)),
            dma((3,)),
            dma((3,)),
            dma((3,)),
            dma((3,)),
            dma((3,)),
            dma,
            dma,
        ],
        compiler_params=pltpu.CompilerParams(collective_id=0, has_side_effects=True),
    )(*args)


def solution(mesh):
    return jax.shard_map(
        lambda *args: tuple(local(*args)),
        mesh=mesh,
        in_specs=(
            P("freq"),
            P("dom", None, None),
            P("dom", None, None),
            P("dom", None),
            P("dom", None, None),
            P("dom", None),
            P("freq", None, "dom", None),
            P("freq", None, "dom", None),
            P("dom", None),
        ),
        out_specs=(P("dom", None), P("dom", None)),
        check_vma=False,
    )
```

time: 492 us -> 43.2 us (0.09)
  the two profiles are of different devices: /device:TPU:0 before, /device:TPU:1 now
where the time goes in v1:
time: 43.2 us; the launch traced here: 43 us
  Pallas kernels  36.8 us (85%)
  local copies, waits for them, and re-layouts  5.55 us (13%)
  between operations  0.65 us (2%)
    pallas_call x1, Pallas kernels, local(): pl.pallas_call(kernel, out_shape=outs, in_specs=[pl.BlockSpec(memory_spac...  36.8 us
    unnamed x9, local copies, waits for them, and re-layouts  5.55 us

profile of v1, /device:TPU:1, one launch (start us, length us, event | category | flops | bytes accessed | tf_op | source)
XLA Modules:
  0.0 43.0 jit_solution(9487588663309183460)
XLA Ops:
  0.6 1.4 %copy.13.edges_hbm = s32[1,6,1024]{2,1,0:T(8,128)} copy(s32[1,6,1024]{2,0,1:T(1,128)} %param.13) | data formatting | bytes 49152 | tf_op args[4]
  2.0 0.0 copy-start
  2.0 1.6 %copy.11.stiffness_hbm = f32[1,36,1024]{2,1,0:T(8,128)} copy(f32[1,36,1024]{2,0,1:T(1,128)} %param.10) | data formatting | bytes 294912 | tf_op args[1]
  3.6 0.0 copy-done
  3.6 0.7 %copy.12.mass_hbm = f32[1,36,1024]{2,1,0:T(8,128)} copy(f32[1,36,1024]{2,0,1:T(1,128)S(1)} %copy-done) | data formatting | bytes 294912 | tf_op args[2]
  4.3 36.8 %shard_map.104 = (f32[1,1024]{1,0:T(1,128)}, f32[1,1024]{1,0:T(1,128)}) custom-call(f32[2]{0:T(128)} %angular.1, f32[1,36,1024]{2,1,0:T(8,128)} %copy.11.stiffness_hbm, f32[1,36,1024]{2,1,0:T(8,128)} %copy.12.mass_hbm, f32[1,1024]{1,0:T(1,128)} %conductivity_hbm.1, s32[1,6,1024]{2,1,0:T(8,128)} %copy.13.edges_hbm, s32[1,1024]{1,0:T(1,128)} %live_hbm.1, ...), custom_call_target="tpu_custom_call" | custom-call | tf_op jit(solution)/shard_map/pallas_call | solution.py:416
  41.1 0.0 copy-start.1
  41.1 1.3 %copy.16 = f32[1,1024]{1,0:T(1,128)} copy(f32[1,1024]{1,0:T(1,128)} %get-tuple-element.4) | data formatting | bytes 8192
  42.4 0.0 copy-done.1
  42.4 0.6 %copy.17 = f32[1,1024]{1,0:T(1,128)} copy(f32[1,1024]{1,0:T(1,128)S(1)} %copy-done.1) | data formatting | bytes 8192
Async XLA Ops:
  2.0 1.6 %copy-start = (f32[1,36,1024]{2,0,1:T(1,128)S(1)}, f32[1,36,1024]{2,0,1:T(1,128)}, u32[]{:S(2)}) copy-start(f32[1,36,1024]{2,0,1:T(1,128)} %param.11) | copy-start | bytes 442372
  41.1 1.3 %copy-start.1 = (f32[1,1024]{1,0:T(1,128)S(1)}, f32[1,1024]{1,0:T(1,128)}, u32[]{:S(2)}) copy-start(f32[1,1024]{1,0:T(1,128)} %get-tuple-element.5) | copy-start | bytes 12292

commit v2 on v1

v2 whole, which is shorter than its diff:
```python
import jax
import jax.numpy as jnp
from jax import lax
from jax.experimental import pallas as pl
from jax.experimental.pallas import tpu as pltpu
from jax.sharding import PartitionSpec as P

MESH = pl.DeviceIdType.MESH
F32 = jnp.float32
BF16 = jnp.bfloat16
DOM = 32
FREQ = 8
RIM = 256
EDGES = 1280
CHUNKS = EDGES // 128
GROUPS = 4
PARTS = 2
STACK = 8 * PARTS


def rows_iota(shape):
    return lax.broadcasted_iota(jnp.int32, shape, 0)


def lanes_iota(shape):
    return lax.broadcasted_iota(jnp.int32, shape, 1)


def lane_pick(table, lane):
    return jnp.take_along_axis(table, lane, axis=1, mode="promise_in_bounds")


def spread(row):
    return jnp.broadcast_to(row, (8, 128))


def chunk(field, c):
    return field[:, 128 * c : 128 * (c + 1)]


def field_rows(ref):
    out = jnp.broadcast_to(ref[0, 0], (8, EDGES))
    kind = rows_iota((8, EDGES)) % 4
    for v in range(1, 4):
        out = jnp.where(kind == v, jnp.broadcast_to(ref[v // 2, v % 2], (8, EDGES)), out)
    return out


def permuted(rim, order):
    out = []
    for q in range(2):
        index = chunk(order, q)
        lane = index & 127
        low = lane_pick(rim[:, :128], lane)
        high = lane_pick(rim[:, 128:], lane)
        out.append(jnp.where(index < 128, low, high))
    return jnp.concatenate(out, axis=1)


def pick(field, index):
    lane = index & 127
    found = [lane_pick(chunk(field, c), lane) for c in range(CHUNKS)]
    bit = 7
    while len(found) > 1:
        odd = (index & (1 << bit)) != 0
        merged = [jnp.where(odd, found[n + 1], found[n]) for n in range(0, len(found) - 1, 2)]
        if len(found) % 2:
            merged.append(found[-1])
        found = merged
        bit += 1
    return found[0]


def edge_dot(a, b, own=None):
    total = chunk(a, 2) * chunk(b, 2)
    for c in range(3, CHUNKS):
        total = total + chunk(a, c) * chunk(b, c)
    rim = chunk(a, 0) * chunk(b, 0) + chunk(a, 1) * chunk(b, 1)
    return total + (rim if own is None else own * rim)


def kernel(
    angular_hbm,
    stiffness_hbm,
    mass_hbm,
    conductivity_hbm,
    edges_hbm,
    live_hbm,
    source_hbm,
    forward_hbm,
    order_hbm,
    total_ref,
    angular,
    stiffness,
    mass,
    conductivity,
    edges,
    live,
    source,
    forward,
    order,
    ids,
    masks,
    onehot,
    blocks,
    weight,
    values,
    down_out,
    up_out,
    down_in,
    up_in,
    sums,
    terms,
    load_sem,
    down_send,
    down_recv,
    up_send,
    up_recv,
    sum_send,
    sum_recv,
    term_send,
    term_recv,
):
    me = lax.axis_index("dom")
    my_freq = lax.axis_index("freq")
    below = lax.rem(me + DOM - 1, DOM)
    above = lax.rem(me + 1, DOM)

    loads = [
        pltpu.make_async_copy(src, dst, load_sem.at[n])
        for n, (src, dst) in enumerate(
            [
                (source_hbm, source),
                (order_hbm, order),
                (edges_hbm, edges),
                (forward_hbm, forward),
                (stiffness_hbm, stiffness),
                (mass_hbm, mass),
                (conductivity_hbm, conductivity),
                (live_hbm, live),
                (angular_hbm, angular),
            ]
        )
    ]
    for load in loads:
        load.start()

    barrier = pltpu.get_barrier_semaphore()
    for k in range(1, DOM):
        peer = lax.rem(me + k, DOM)
        pl.semaphore_signal(barrier, inc=1, device_id=(my_freq, peer), device_id_type=MESH)
    for k in range(1, FREQ):
        peer = lax.rem(my_freq + k, FREQ)
        pl.semaphore_signal(barrier, inc=1, device_id=(peer, me), device_id_type=MESH)

    lane = lanes_iota((8, 128))
    sub = rows_iota((8, 128))
    upper = sub < 4

    def halves(ref, n, q):
        first = ref[n, :, pl.ds(pl.multiple_of(128 * q, 128), 128)]
        second = ref[n, :, pl.ds(pl.multiple_of(512 + 128 * q, 128), 128)]
        return jnp.where(upper, spread(first), spread(second))

    loads[0].wait()
    loads[1].wait()
    order_rows = jnp.broadcast_to(order[...], (8, RIM))
    match = jnp.where(rows_iota((RIM, RIM)) == jnp.broadcast_to(order[...], (RIM, RIM)), 1.0, 0.0)
    inverse = lax.dot_general(
        lanes_iota((8, RIM)).astype(F32).astype(BF16),
        match.astype(BF16),
        (((1,), (1,)), ((), ())),
        preferred_element_type=F32,
    ).astype(jnp.int32)
    sources = field_rows(source)

    loads[2].wait()

    def tables(q, carry):
        for i in range(6):
            index = halves(edges, i, q)
            ids[q, i] = index
            wide = index >> 7
            for c in range(CHUNKS):
                hit = jnp.where(wide == c, 1.0, 0.0)
                masks[q, c, :, 128 * i : 128 * (i + 1)] = jnp.concatenate([hit] * PARTS, axis=0).astype(BF16)
        for h in range(2):
            at = pl.ds(pl.multiple_of(512 * h + 128 * q, 128), 128)
            stacked = spread(edges[0, :, at])
            for i in range(1, 6):
                stacked = jnp.where(sub == i, spread(edges[i, :, at]), stacked)
            columns = jnp.transpose(stacked & 127)
            for i in range(6):
                hit = jnp.broadcast_to(columns[:, i : i + 1], (128, 128)) == lanes_iota((128, 128))
                onehot[q, 128 * i : 128 * (i + 1), 128 * h : 128 * (h + 1)] = jnp.where(hit, 1.0, 0.0).astype(BF16)
        return carry

    lax.fori_loop(0, GROUPS, tables, 0)

    def send_rims(k, field):
        down_out[k] = permuted(field[:, :RIM], inverse)
        up_out[k] = field[:, EDGES - RIM :]
        copies = (
            pltpu.make_async_remote_copy(
                src_ref=down_out.at[k],
                dst_ref=down_in.at[k],
                send_sem=down_send.at[k],
                recv_sem=down_recv.at[k],
                device_id=(my_freq, below),
                device_id_type=MESH,
            ),
            pltpu.make_async_remote_copy(
                src_ref=up_out.at[k],
                dst_ref=up_in.at[k],
                send_sem=up_send.at[k],
                recv_sem=up_recv.at[k],
                device_id=(my_freq, above),
                device_id_type=MESH,
            ),
        )
        for copy in copies:
            copy.start()
        return copies

    def join_rims(k, copies, field):
        for copy in copies:
            copy.wait_recv()
        zero = jnp.zeros((8, RIM), F32)
        from_below = jnp.where(me > 0, permuted(up_in[k], order_rows), zero)
        from_above = jnp.where(me < DOM - 1, down_in[k], zero)
        return jnp.concatenate(
            [
                field[:, :RIM] + from_below,
                field[:, RIM : EDGES - RIM],
                field[:, EDGES - RIM :] + from_above,
            ],
            axis=1,
        )

    pl.semaphore_wait(barrier, DOM - 1 + FREQ - 1)
    rims0 = send_rims(0, sources)

    for n in range(3, 9):
        loads[n].wait()
    omega = jnp.where(sub % 4 < 2, angular[0], angular[1])
    forwards = field_rows(forward)

    def elements(q, carry):
        alive = halves(live, 0, q).astype(F32)
        shift = omega * (halves(conductivity, 0, q) * alive)
        picked = [pick(forwards, ids[q, j]) for j in range(6)]
        for i in range(6):
            running = None
            for j in range(6):
                n = 6 * i + j
                mass_rows = halves(mass, n, q)
                blocks[q, n] = halves(stiffness, n, q) * alive + shift * mass_rows
                product = mass_rows * picked[j]
                running = product if running is None else running + product
            weight[q, i] = omega * running
        return carry

    lax.fori_loop(0, GROUPS, elements, 0)

    def apply(field):
        out = None
        terms_of = []
        for q in range(GROUPS):
            picked = [pick(field, ids[q, i]) for i in range(6)]
            term = weight[q, 0] * picked[0]
            for i in range(1, 6):
                term = term + weight[q, i] * picked[i]
            terms_of.append(term)
            for i in range(6):
                running = blocks[q, 6 * i] * picked[0]
                for j in range(1, 6):
                    running = running + blocks[q, 6 * i + j] * picked[j]
                pieces = []
                rest = running
                for _ in range(PARTS - 1):
                    head = rest.astype(BF16).astype(F32)
                    pieces.append(head)
                    rest = rest - head
                pieces.append(rest)
                stacked = jnp.concatenate(pieces, axis=0).astype(BF16)
                for c in range(CHUNKS):
                    values[q, STACK * c : STACK * (c + 1), 128 * i : 128 * (i + 1)] = (
                        stacked * masks[q, c, :, 128 * i : 128 * (i + 1)]
                    )
            product = lax.dot_general(
                values[q], onehot[q], (((1,), (0,)), ((), ())), preferred_element_type=F32
            )
            out = product if out is None else out + product
        pieces = []
        for c in range(CHUNKS):
            both = out[STACK * c : STACK * c + 8]
            for s in range(1, PARTS):
                both = both + out[STACK * c + 8 * s : STACK * c + 8 * s + 8]
            mixed = jnp.where(upper, both[:, :128], both[:, 128:])
            pieces.append(mixed + pltpu.roll(mixed, 4, 0))
        return jnp.concatenate(pieces, axis=1), jnp.concatenate(terms_of, axis=1)

    def send_sums(k, quantities):
        row = jnp.zeros((8, 128), F32)
        for n, quantity in enumerate(quantities):
            column = jnp.sum(quantity, axis=1, keepdims=True)
            row = row + jnp.where((lane == 4 * n + sub) & upper, column, 0.0)
        sums[k, me] = jnp.sum(row, axis=0, keepdims=True)
        for n in range(1, DOM):
            peer = lax.rem(me + n, DOM)
            pltpu.make_async_remote_copy(
                src_ref=sums.at[k, me],
                dst_ref=sums.at[k, me],
                send_sem=sum_send.at[k],
                recv_sem=sum_recv.at[k],
                device_id=(my_freq, peer),
                device_id_type=MESH,
            ).start()

    def take_sums(k, count):
        rest = sums.at[k, pl.ds(0, DOM - 1)]
        pltpu.make_async_copy(rest, rest, sum_recv.at[k]).wait()
        total = spread(jnp.sum(sums[k], axis=0))
        return [
            jnp.sum(jnp.where(lane == 4 * n + sub % 4, total, 0.0), axis=1, keepdims=True)
            for n in range(count)
        ]

    own = jnp.where(me > 0, 0.0, 1.0).astype(F32)

    base = join_rims(0, rims0, sources)
    image0, term0 = apply(base)
    rims1 = send_rims(1, image0)
    send_sums(0, [edge_dot(base, base, own), edge_dot(base, image0)])
    first = join_rims(1, rims1, image0)
    image1, term1 = apply(first)
    rims2 = send_rims(2, image1)

    norm0, curve0 = take_sums(0, 2)
    alpha0 = norm0 / curve0
    residual1 = base - alpha0 * first
    local1 = image0 - alpha0 * image1
    send_sums(
        1,
        [
            edge_dot(residual1, residual1, own),
            edge_dot(residual1, local1),
            edge_dot(residual1, image0) + edge_dot(base, local1),
        ],
    )
    second = join_rims(2, rims2, image1)
    image2, term2 = apply(second)

    norm1, self1, cross1 = take_sums(1, 3)
    beta0 = norm1 / norm0
    curve1 = self1 + beta0 * cross1 + (beta0 * beta0) * curve0
    alpha1 = norm1 / curve1
    direction1 = residual1 + beta0 * base
    along1 = local1 + beta0 * image0
    residual2 = residual1 - alpha1 * ((first - alpha0 * second) + beta0 * first)
    local2 = local1 - alpha1 * ((image1 - alpha0 * image2) + beta0 * image1)
    send_sums(
        2,
        [
            edge_dot(residual2, residual2, own),
            edge_dot(residual2, local2),
            edge_dot(residual2, along1) + edge_dot(direction1, local2),
        ],
    )
    near1 = term0 - alpha0 * term1
    toward1 = near1 + beta0 * term0
    near2 = near1 - alpha1 * ((term1 - alpha0 * term2) + beta0 * term1)
    so_far = alpha0 * term0 + alpha1 * toward1

    norm2, self2, cross2 = take_sums(2, 3)
    beta1 = norm2 / norm1
    curve2 = self2 + beta1 * cross2 + (beta1 * beta1) * curve1
    alpha2 = norm2 / curve2
    total = so_far + alpha2 * (near2 + beta1 * toward1)

    total = total + pltpu.roll(total, 1, 0)
    total = total + pltpu.roll(total, 2, 0)
    packed = jnp.zeros((8, 128), F32)
    for h in range(2):
        for q in range(GROUPS):
            piece = spread(total[4 * h + 3 : 4 * h + 4, 128 * q : 128 * (q + 1)])
            packed = jnp.where(sub == 4 * h + q, piece, packed)
    terms[my_freq] = packed
    for n in range(1, FREQ):
        peer = lax.rem(my_freq + n, FREQ)
        pltpu.make_async_remote_copy(
            src_ref=terms.at[my_freq],
            dst_ref=terms.at[my_freq],
            send_sem=term_send,
            recv_sem=term_recv,
            device_id=(peer, me),
            device_id_type=MESH,
        ).start()
    for copy in rims0 + rims1 + rims2:
        copy.wait_send()
    for k in range(3):
        sent = sums.at[k, pl.ds(0, DOM - 1)]
        pltpu.make_async_copy(sent, sent, sum_send.at[k]).wait()
    rest = terms.at[pl.ds(0, FREQ - 1)]
    pltpu.make_async_copy(rest, rest, term_recv).wait()
    added = terms[0]
    for n in range(1, FREQ):
        added = added + terms[n]
    for r in range(8):
        total_ref[:, 128 * r : 128 * (r + 1)] = added[r : r + 1]
    pltpu.make_async_copy(rest, rest, term_send).wait()


def local(
    angular,
    stiffness,
    mass_matrix,
    conductivity,
    element_edges,
    live_slots,
    adjoint_source,
    forward_field,
    neighbour_map,
):
    hbm = pl.BlockSpec(memory_space=pltpu.MemorySpace.HBM)
    dma = pltpu.SemaphoreType.DMA
    total = pl.pallas_call(
        kernel,
        out_shape=jax.ShapeDtypeStruct((1, 1024), F32),
        in_specs=[hbm] * 9,
        out_specs=pl.BlockSpec(memory_space=pltpu.MemorySpace.VMEM),
        scratch_shapes=[
            pltpu.SMEM((2,), F32),
            pltpu.VMEM((36, 1, 1024), F32),
            pltpu.VMEM((36, 1, 1024), F32),
            pltpu.VMEM((1, 1, 1024), F32),
            pltpu.VMEM((6, 1, 1024), jnp.int32),
            pltpu.VMEM((1, 1, 1024), jnp.int32),
            pltpu.VMEM((2, 2, 1, EDGES), F32),
            pltpu.VMEM((2, 2, 1, EDGES), F32),
            pltpu.VMEM((1, RIM), jnp.int32),
            pltpu.VMEM((GROUPS, 6, 8, 128), jnp.int32),
            pltpu.VMEM((GROUPS, CHUNKS, STACK, 768), BF16),
            pltpu.VMEM((GROUPS, 768, 256), BF16),
            pltpu.VMEM((GROUPS, 36, 8, 128), F32),
            pltpu.VMEM((GROUPS, 6, 8, 128), F32),
            pltpu.VMEM((GROUPS, STACK * CHUNKS, 768), BF16),
            pltpu.VMEM((3, 8, RIM), F32),
            pltpu.VMEM((3, 8, RIM), F32),
            pltpu.VMEM((3, 8, RIM), F32),
            pltpu.VMEM((3, 8, RIM), F32),
            pltpu.VMEM((3, DOM, 1, 128), F32),
            pltpu.VMEM((FREQ, 8, 128), F32),
            dma((9,)),
            dma((3,)),
            dma((3,)),
            dma((3,)),
            dma((3,)),
            dma((3,)),
            dma((3,)),
            dma,
            dma,
        ],
        compiler_params=pltpu.CompilerParams(collective_id=0, has_side_effects=True),
    )(
        angular,
        jnp.transpose(stiffness, (1, 0, 2)),
        jnp.transpose(mass_matrix, (1, 0, 2)),
        conductivity[None],
        jnp.transpose(element_edges, (1, 0, 2)),
        live_slots[None],
        adjoint_source,
        forward_field,
        neighbour_map,
    )
    gradient = -total * live_slots.astype(F32)
    updated = conductivity * jnp.exp(-0.5 * jnp.tanh(gradient))
    return gradient, updated


def solution(mesh):
    return jax.shard_map(
        local,
        mesh=mesh,
        in_specs=(
            P("freq"),
            P("dom", None, None),
            P("dom", None, None),
            P("dom", None),
            P("dom", None, None),
            P("dom", None),
            P("freq", None, "dom", None),
            P("freq", None, "dom", None),
            P("dom", None),
        ),
        out_specs=(P("dom", None), P("dom", None)),
        check_vma=False,
    )
```

time: 43.2 us -> 36.8 us (0.85)
  local copies, waits for them, and re-layouts: 5.55 us -> 0.01 us
  Pallas kernels: 36.8 us -> 34.7 us
  other arithmetic: 0 us -> 1.3 us
    unnamed x9 -> x4, local copies, waits for them, and re-layouts: 5.55 us -> 0.01 us
    pallas_call x1, Pallas kernels: 36.8 us -> 34.7 us  [local(): pl.pallas_call(kernel, out_shape=jax.ShapeDtypeStruct((1, 1024), F32), in...]
    mul x0 -> x1, other arithmetic: none -> 1.3 us  [local(): updated = conductivity * jnp.exp(-0.5 * jnp.tanh(gradient))]
where the time goes in v2:
time: 36.8 us; the launch traced here: 36.7 us
  Pallas kernels  34.7 us (94%)
  other arithmetic  1.3 us (4%)
  between operations  0.67 us (2%)
    pallas_call x1, Pallas kernels, local(): pl.pallas_call(kernel, out_shape=jax.ShapeDtypeStruct((1, 1024), F32), in...  34.7 us
    mul x1, other arithmetic, local(): updated = conductivity * jnp.exp(-0.5 * jnp.tanh(gradient))  1.3 us

profile of v2, /device:TPU:1, one launch (start us, length us, event | category | flops | bytes accessed | tf_op | source)
XLA Modules:
  0.0 36.7 jit_solution(16073752198945004831)
XLA Ops:
  0.6 0.0 copy-start
  0.6 0.0 copy-start.1
  0.7 34.7 %shard_map.104 = f32[1,1024]{1,0:T(1,128)} custom-call(f32[2]{0:T(128)} %angular_hbm.1, f32[36,1,1024]{2,1,0:T(1,128)} %bitcast.5, f32[36,1,1024]{2,1,0:T(1,128)} %bitcast.6, f32[1,1,1024]{2,1,0:T(1,128)} %bitcast.8, s32[6,1,1024]{2,1,0:T(1,128)} %bitcast.7, s32[1,1,1024]{2,1,0:T(1,128)} %bitcast.9, f32[2,2,1,1280]{3,2,1,0:T(1,128)} %source_hbm.1, ...), custom_call_target="tpu_custom_call" | custom-call | tf_op jit(solution)/shard_map/pallas_call | solution.py:427
  35.4 0.0 copy-done
  35.4 0.0 copy-done.1
  35.4 1.3 %exponential_multiply_fusion = (f32[1,1024]{1,0:T(1,128)}, f32[1,1024]{1,0:T(1,128)}) fusion(f32[1,1024]{1,0:T(1,128)S(1)} %copy-done, s32[1,1024]{1,0:T(1,128)S(1)} %copy-done.1, f32[1,1024]{1,0:T(1,128)} %shard_map.104), kind=kLoop, calls=%fused_computation | loop fusion | flops 5120 | bytes 20480 | tf_op jit(solution)/shard_map/mul | solution.py:477
Async XLA Ops:
  0.6 34.7 %copy-start = (f32[1,1024]{1,0:T(1,128)S(1)}, f32[1,1024]{1,0:T(1,128)}, u32[]{:S(2)}) copy-start(f32[1,1024]{1,0:T(1,128)} %param.12) | copy-start | bytes 12292
  0.6 34.7 %copy-start.1 = (s32[1,1024]{1,0:T(1,128)S(1)}, s32[1,1024]{1,0:T(1,128)}, u32[]{:S(2)}) copy-start(s32[1,1024]{1,0:T(1,128)} %param.14) | copy-start | bytes 12292

commit v3 on v2

--- a/solution.py
+++ b/solution.py
@@ -16,6 +16,9 @@
 GROUPS = 4
 PARTS = 2
 STACK = 8 * PARTS
+HOPS = (0, 1, 2, 1)
+DOM_PEERS = sorted(range(1, DOM), key=lambda k: (-HOPS[k // 8] - HOPS[k // 2 % 4], k))
+FREQ_PEERS = (4, 3, 5, 2, 6, 1, 7)
 
 
 def rows_iota(shape):
@@ -146,10 +149,9 @@
         load.start()
 
     barrier = pltpu.get_barrier_semaphore()
-    for k in range(1, DOM):
-        peer = lax.rem(me + k, DOM)
-        pl.semaphore_signal(barrier, inc=1, device_id=(my_freq, peer), device_id_type=MESH)
-    for k in range(1, FREQ):
+    for k in DOM_PEERS:
+        pl.semaphore_signal(barrier, inc=1, device_id=(my_freq, me ^ k), device_id_type=MESH)
+    for k in FREQ_PEERS:
         peer = lax.rem(my_freq + k, FREQ)
         pl.semaphore_signal(barrier, inc=1, device_id=(peer, me), device_id_type=MESH)
 
@@ -196,6 +198,14 @@
         return carry
 
     lax.fori_loop(0, GROUPS, tables, 0)
+
+    @pl.when(me == 0)
+    def _():
+        up_in[...] = jnp.zeros((3, 8, RIM), F32)
+
+    @pl.when(me == DOM - 1)
+    def _():
+        down_in[...] = jnp.zeros((3, 8, RIM), F32)
 
     def send_rims(k, field):
         down_out[k] = permuted(field[:, :RIM], inverse)
@@ -218,21 +228,18 @@
                 device_id_type=MESH,
             ),
         )
-        for copy in copies:
-            copy.start()
+        pl.when(me > 0)(copies[0].start)
+        pl.when(me < DOM - 1)(copies[1].start)
         return copies
 
     def join_rims(k, copies, field):
-        for copy in copies:
-            copy.wait_recv()
-        zero = jnp.zeros((8, RIM), F32)
-        from_below = jnp.where(me > 0, permuted(up_in[k], order_rows), zero)
-        from_above = jnp.where(me < DOM - 1, down_in[k], zero)
+        pl.when(me < DOM - 1)(copies[0].wait_recv)
+        pl.when(me > 0)(copies[1].wait_recv)
         return jnp.concatenate(
             [
-                field[:, :RIM] + from_below,
+                field[:, :RIM] + permuted(up_in[k], order_rows),
                 field[:, RIM : EDGES - RIM],
-                field[:, EDGES - RIM :] + from_above,
+                field[:, EDGES - RIM :] + down_in[k],
             ],
             axis=1,
         )
@@ -306,14 +313,13 @@
             column = jnp.sum(quantity, axis=1, keepdims=True)
             row = row + jnp.where((lane == 4 * n + sub) & upper, column, 0.0)
         sums[k, me] = jnp.sum(row, axis=0, keepdims=True)
-        for n in range(1, DOM):
-            peer = lax.rem(me + n, DOM)
+        for n in DOM_PEERS:
             pltpu.make_async_remote_copy(
                 src_ref=sums.at[k, me],
                 dst_ref=sums.at[k, me],
                 send_sem=sum_send.at[k],
                 recv_sem=sum_recv.at[k],
-                device_id=(my_freq, peer),
+                device_id=(my_freq, me ^ n),
                 device_id_type=MESH,
             ).start()
 
@@ -338,45 +344,42 @@
 
     norm0, curve0 = take_sums(0, 2)
     alpha0 = norm0 / curve0
-    residual1 = base - alpha0 * first
-    local1 = image0 - alpha0 * image1
-    send_sums(
-        1,
-        [
-            edge_dot(residual1, residual1, own),
-            edge_dot(residual1, local1),
-            edge_dot(residual1, image0) + edge_dot(base, local1),
-        ],
+    residual = base - alpha0 * first
+    residual_image = image0 - alpha0 * image1
+    early = [
+        edge_dot(residual, residual, own),
+        edge_dot(residual, residual_image),
+        edge_dot(base, residual_image),
+        edge_dot(first, first, own),
+        edge_dot(first, image1),
+    ]
+    near = term0 - alpha0 * term1
+    second = join_rims(2, rims2, image1)
+    turned = first - alpha0 * second
+    early += [edge_dot(turned, turned, own), edge_dot(first, turned, own)]
+    image2, term2 = apply(second)
+    turned_image = image1 - alpha0 * image2
+    send_sums(1, early + [edge_dot(turned, turned_image), edge_dot(first, turned_image)])
+    far = term1 - alpha0 * term2
+
+    norm1, rr1, br1, bb2, bb3, rr2, br2, rr3, br3 = take_sums(1, 9)
+    beta0 = norm1 / norm0
+    along1 = rr1 + beta0 * br1
+    curve1 = along1 + beta0 * (br1 + beta0 * curve0)
+    alpha1 = norm1 / curve1
+    square = rr2 + beta0 * (2.0 * br2 + beta0 * bb2)
+    norm2 = norm1 - alpha1 * (2.0 * along1 - alpha1 * square)
+    self2 = rr1 - alpha1 * (2.0 * (rr2 + beta0 * br2) - alpha1 * (rr3 + beta0 * (2.0 * br3 + beta0 * bb3)))
+    cross2 = along1 - alpha1 * square
+    beta1 = norm2 / norm1
+    curve2 = self2 + beta1 * (2.0 * cross2 + beta1 * curve1)
+    alpha2 = norm2 / curve2
+    on_d1 = alpha1 + alpha2 * beta1
+    total = (
+        (alpha0 + on_d1 * beta0) * term0
+        + (on_d1 + alpha2) * near
+        - (alpha2 * alpha1) * (far + beta0 * term1)
     )
-    second = join_rims(2, rims2, image1)
-    image2, term2 = apply(second)
-
-    norm1, self1, cross1 = take_sums(1, 3)
-    beta0 = norm1 / norm0
-    curve1 = self1 + beta0 * cross1 + (beta0 * beta0) * curve0
-    alpha1 = norm1 / curve1
-    direction1 = residual1 + beta0 * base
-    along1 = local1 + beta0 * image0
-    residual2 = residual1 - alpha1 * ((first - alpha0 * second) + beta0 * first)
-    local2 = local1 - alpha1 * ((image1 - alpha0 * image2) + beta0 * image1)
-    send_sums(
-        2,
-        [
-            edge_dot(residual2, residual2, own),
-            edge_dot(residual2, local2),
-            edge_dot(residual2, along1) + edge_dot(direction1, local2),
-        ],
-    )
-    near1 = term0 - alpha0 * term1
-    toward1 = near1 + beta0 * term0
-    near2 = near1 - alpha1 * ((term1 - alpha0 * term2) + beta0 * term1)
-    so_far = alpha0 * term0 + alpha1 * toward1
-
-    norm2, self2, cross2 = take_sums(2, 3)
-    beta1 = norm2 / norm1
-    curve2 = self2 + beta1 * cross2 + (beta1 * beta1) * curve1
-    alpha2 = norm2 / curve2
-    total = so_far + alpha2 * (near2 + beta1 * toward1)
 
     total = total + pltpu.roll(total, 1, 0)
     total = total + pltpu.roll(total, 2, 0)
@@ -386,7 +389,7 @@
             piece = spread(total[4 * h + 3 : 4 * h + 4, 128 * q : 128 * (q + 1)])
             packed = jnp.where(sub == 4 * h + q, piece, packed)
     terms[my_freq] = packed
-    for n in range(1, FREQ):
+    for n in FREQ_PEERS:
         peer = lax.rem(my_freq + n, FREQ)
         pltpu.make_async_remote_copy(
             src_ref=terms.at[my_freq],
@@ -396,9 +399,10 @@
             device_id=(peer, me),
             device_id_type=MESH,
         ).start()
-    for copy in rims0 + rims1 + rims2:
-        copy.wait_send()
-    for k in range(3):
+    for copies in (rims0, rims1, rims2):
+        pl.when(me > 0)(copies[0].wait_send)
+        pl.when(me < DOM - 1)(copies[1].wait_send)
+    for k in range(2):
         sent = sums.at[k, pl.ds(0, DOM - 1)]
         pltpu.make_async_copy(sent, sent, sum_send.at[k]).wait()
     rest = terms.at[pl.ds(0, FREQ - 1)]
@@ -449,7 +453,7 @@
             pltpu.VMEM((3, 8, RIM), F32),
             pltpu.VMEM((3, 8, RIM), F32),
             pltpu.VMEM((3, 8, RIM), F32),
-            pltpu.VMEM((3, DOM, 1, 128), F32),
+            pltpu.VMEM((2, DOM, 1, 128), F32),
             pltpu.VMEM((FREQ, 8, 128), F32),
             dma((9,)),
             dma((3,)),

time: 36.8 us -> 34 us (0.924)
  Pallas kernels: 34.7 us -> 31.9 us
    pallas_call x1, Pallas kernels: 34.7 us -> 31.9 us  [local(): pl.pallas_call(kernel, out_shape=jax.ShapeDtypeStruct((1, 1024), F32), in...]
where the time goes in v3:
time: 34 us; the launch traced here: 33.9 us
  Pallas kernels  31.9 us (94%)
  other arithmetic  1.3 us (4%)
  between operations  0.67 us (2%)
    pallas_call x1, Pallas kernels, local(): pl.pallas_call(kernel, out_shape=jax.ShapeDtypeStruct((1, 1024), F32), in...  31.9 us
    mul x1, other arithmetic, local(): updated = conductivity * jnp.exp(-0.5 * jnp.tanh(gradient))  1.3 us

profile of v3, /device:TPU:1, one launch (start us, length us, event | category | flops | bytes accessed | tf_op | source)
XLA Modules:
  0.0 33.9 jit_solution(3353809790302401018)
XLA Ops:
  0.6 0.0 copy-start
  0.6 0.0 copy-start.1
  0.7 31.9 %shard_map.104 = f32[1,1024]{1,0:T(1,128)} custom-call(f32[2]{0:T(128)} %angular_hbm.1, f32[36,1,1024]{2,1,0:T(1,128)} %bitcast.5, f32[36,1,1024]{2,1,0:T(1,128)} %bitcast.6, f32[1,1,1024]{2,1,0:T(1,128)} %bitcast.8, s32[6,1,1024]{2,1,0:T(1,128)} %bitcast.7, s32[1,1,1024]{2,1,0:T(1,128)} %bitcast.9, f32[2,2,1,1280]{3,2,1,0:T(1,128)} %source_hbm.1, ...), custom_call_target="tpu_custom_call" | custom-call | tf_op jit(solution)/shard_map/pallas_call | solution.py:431
  32.6 0.0 copy-done
  32.6 0.0 copy-done.1
  32.6 1.3 %exponential_multiply_fusion = (f32[1,1024]{1,0:T(1,128)}, f32[1,1024]{1,0:T(1,128)}) fusion(f32[1,1024]{1,0:T(1,128)S(1)} %copy-done, s32[1,1024]{1,0:T(1,128)S(1)} %copy-done.1, f32[1,1024]{1,0:T(1,128)} %shard_map.104), kind=kLoop, calls=%fused_computation | loop fusion | flops 5120 | bytes 20480 | tf_op jit(solution)/shard_map/mul | solution.py:481
Async XLA Ops:
  0.6 32.0 %copy-start = (f32[1,1024]{1,0:T(1,128)S(1)}, f32[1,1024]{1,0:T(1,128)}, u32[]{:S(2)}) copy-start(f32[1,1024]{1,0:T(1,128)} %param.12) | copy-start | bytes 12292
  0.6 32.0 %copy-start.1 = (s32[1,1024]{1,0:T(1,128)S(1)}, s32[1,1024]{1,0:T(1,128)}, u32[]{:S(2)}) copy-start(s32[1,1024]{1,0:T(1,128)} %param.14) | copy-start | bytes 12292

commit v4 on v3

--- a/solution.py
+++ b/solution.py
@@ -19,6 +19,9 @@
 HOPS = (0, 1, 2, 1)
 DOM_PEERS = sorted(range(1, DOM), key=lambda k: (-HOPS[k // 8] - HOPS[k // 2 % 4], k))
 FREQ_PEERS = (4, 3, 5, 2, 6, 1, 7)
+NEAR = [k for k in range(1, DOM) if HOPS[k // 8] + HOPS[k // 2 % 4] <= 1]
+ONE_HOP = [k for k in NEAR if k % 2 == 0]
+TWO_HOPS = [k for k in range(0, DOM, 2) if HOPS[k // 8] + HOPS[k // 2 % 4] == 2]
 
 
 def rows_iota(shape):
@@ -123,6 +126,8 @@
     sum_recv,
     term_send,
     term_recv,
+    round_two,
+    round_three,
 ):
     me = lax.axis_index("dom")
     my_freq = lax.axis_index("freq")
@@ -149,11 +154,20 @@
         load.start()
 
     barrier = pltpu.get_barrier_semaphore()
-    for k in DOM_PEERS:
-        pl.semaphore_signal(barrier, inc=1, device_id=(my_freq, me ^ k), device_id_type=MESH)
-    for k in FREQ_PEERS:
-        peer = lax.rem(my_freq + k, FREQ)
-        pl.semaphore_signal(barrier, inc=1, device_id=(peer, me), device_id_type=MESH)
+    row_end = lax.rem(me, 8) == 7
+    row_start = lax.rem(me, 8) == 0
+    end_pair = row_end & (me < DOM - 1)
+    start_pair = row_start & (me > 0)
+
+    def signal(semaphore, freq, dom):
+        pl.semaphore_signal(semaphore, inc=1, device_id=(freq, dom), device_id_type=MESH)
+
+    pl.when(end_pair)(lambda: signal(barrier, my_freq, above))
+    pl.when(start_pair)(lambda: signal(barrier, my_freq, below))
+    for k in NEAR:
+        signal(barrier, my_freq, me ^ k)
+    for d in (1, 7):
+        signal(barrier, lax.rem(my_freq + d, FREQ), me)
 
     lane = lanes_iota((8, 128))
     sub = rows_iota((8, 128))
@@ -175,29 +189,6 @@
         preferred_element_type=F32,
     ).astype(jnp.int32)
     sources = field_rows(source)
-
-    loads[2].wait()
-
-    def tables(q, carry):
-        for i in range(6):
-            index = halves(edges, i, q)
-            ids[q, i] = index
-            wide = index >> 7
-            for c in range(CHUNKS):
-                hit = jnp.where(wide == c, 1.0, 0.0)
-                masks[q, c, :, 128 * i : 128 * (i + 1)] = jnp.concatenate([hit] * PARTS, axis=0).astype(BF16)
-        for h in range(2):
-            at = pl.ds(pl.multiple_of(512 * h + 128 * q, 128), 128)
-            stacked = spread(edges[0, :, at])
-            for i in range(1, 6):
-                stacked = jnp.where(sub == i, spread(edges[i, :, at]), stacked)
-            columns = jnp.transpose(stacked & 127)
-            for i in range(6):
-                hit = jnp.broadcast_to(columns[:, i : i + 1], (128, 128)) == lanes_iota((128, 128))
-                onehot[q, 128 * i : 128 * (i + 1), 128 * h : 128 * (h + 1)] = jnp.where(hit, 1.0, 0.0).astype(BF16)
-        return carry
-
-    lax.fori_loop(0, GROUPS, tables, 0)
 
     @pl.when(me == 0)
     def _():
@@ -244,8 +235,35 @@
             axis=1,
         )
 
-    pl.semaphore_wait(barrier, DOM - 1 + FREQ - 1)
+    pl.semaphore_wait(barrier, len(NEAR) + 2 + end_pair.astype(jnp.int32) + start_pair.astype(jnp.int32))
     rims0 = send_rims(0, sources)
+    for k in ONE_HOP:
+        signal(round_two, my_freq, me ^ k)
+    for d in (1, 7):
+        signal(round_two, lax.rem(my_freq + d, FREQ), me)
+
+    loads[2].wait()
+
+    def tables(q, carry):
+        for i in range(6):
+            index = halves(edges, i, q)
+            ids[q, i] = index
+            wide = index >> 7
+            for c in range(CHUNKS):
+                hit = jnp.where(wide == c, 1.0, 0.0)
+                masks[q, c, :, 128 * i : 128 * (i + 1)] = jnp.concatenate([hit] * PARTS, axis=0).astype(BF16)
+        for h in range(2):
+            at = pl.ds(pl.multiple_of(512 * h + 128 * q, 128), 128)
+            stacked = spread(edges[0, :, at])
+            for i in range(1, 6):
+                stacked = jnp.where(sub == i, spread(edges[i, :, at]), stacked)
+            columns = jnp.transpose(stacked & 127)
+            for i in range(6):
+                hit = jnp.broadcast_to(columns[:, i : i + 1], (128, 128)) == lanes_iota((128, 128))
+                onehot[q, 128 * i : 128 * (i + 1), 128 * h : 128 * (h + 1)] = jnp.where(hit, 1.0, 0.0).astype(BF16)
+        return carry
+
+    lax.fori_loop(0, GROUPS, tables, 0)
 
     for n in range(3, 9):
         loads[n].wait()
@@ -268,6 +286,12 @@
         return carry
 
     lax.fori_loop(0, GROUPS, elements, 0)
+
+    pl.semaphore_wait(round_two, len(ONE_HOP) + 2)
+    for k in TWO_HOPS:
+        signal(round_three, my_freq, me ^ k)
+    for d in (2, 6):
+        signal(round_three, lax.rem(my_freq + d, FREQ), me)
 
     def apply(field):
         out = None
@@ -337,29 +361,36 @@
     base = join_rims(0, rims0, sources)
     image0, term0 = apply(base)
     rims1 = send_rims(1, image0)
+    first = join_rims(1, rims1, image0)
+    pl.semaphore_wait(round_three, len(TWO_HOPS) + 2)
     send_sums(0, [edge_dot(base, base, own), edge_dot(base, image0)])
-    first = join_rims(1, rims1, image0)
     image1, term1 = apply(first)
     rims2 = send_rims(2, image1)
+
+    second = join_rims(2, rims2, image1)
+    image2, term2 = apply(second)
 
     norm0, curve0 = take_sums(0, 2)
     alpha0 = norm0 / curve0
     residual = base - alpha0 * first
     residual_image = image0 - alpha0 * image1
-    early = [
-        edge_dot(residual, residual, own),
-        edge_dot(residual, residual_image),
-        edge_dot(base, residual_image),
-        edge_dot(first, first, own),
-        edge_dot(first, image1),
-    ]
+    turned = first - alpha0 * second
+    turned_image = image1 - alpha0 * image2
+    send_sums(
+        1,
+        [
+            edge_dot(residual, residual, own),
+            edge_dot(residual, residual_image),
+            edge_dot(base, residual_image),
+            edge_dot(first, first, own),
+            edge_dot(first, image1),
+            edge_dot(turned, turned, own),
+            edge_dot(first, turned, own),
+            edge_dot(turned, turned_image),
+            edge_dot(first, turned_image),
+        ],
+    )
     near = term0 - alpha0 * term1
-    second = join_rims(2, rims2, image1)
-    turned = first - alpha0 * second
-    early += [edge_dot(turned, turned, own), edge_dot(first, turned, own)]
-    image2, term2 = apply(second)
-    turned_image = image1 - alpha0 * image2
-    send_sums(1, early + [edge_dot(turned, turned_image), edge_dot(first, turned_image)])
     far = term1 - alpha0 * term2
 
     norm1, rr1, br1, bb2, bb3, rr2, br2, rr3, br3 = take_sums(1, 9)
@@ -430,7 +461,7 @@
     dma = pltpu.SemaphoreType.DMA
     total = pl.pallas_call(
         kernel,
-        out_shape=jax.ShapeDtypeStruct((1, 1024), F32),
+        out_shape=pltpu.VMEM((1, 1024), F32),
         in_specs=[hbm] * 9,
         out_specs=pl.BlockSpec(memory_space=pltpu.MemorySpace.VMEM),
         scratch_shapes=[
@@ -464,6 +495,8 @@
             dma((3,)),
             dma,
             dma,
+            pltpu.SemaphoreType.REGULAR,
+            pltpu.SemaphoreType.REGULAR,
         ],
         compiler_params=pltpu.CompilerParams(collective_id=0, has_side_effects=True),
     )(

time: 34 us -> 31.9 us (0.938)
  Pallas kernels: 31.9 us -> 30.5 us
  other arithmetic: 1.3 us -> 0.62 us
    pallas_call x1, Pallas kernels: 31.9 us -> 30.5 us  [local(): pl.pallas_call(kernel, out_shape=pltpu.VMEM((1, 1024), F32), in_specs=[hb...]
    mul x1, other arithmetic: 1.3 us -> 0.62 us  [local(): updated = conductivity * jnp.exp(-0.5 * jnp.tanh(gradient))]
where the time goes in v4:
time: 31.9 us; the launch traced here: 31.8 us
  Pallas kernels  30.5 us (96%)
  between operations  0.67 us (2%)
  other arithmetic  0.62 us (2%)
    pallas_call x1, Pallas kernels, local(): pl.pallas_call(kernel, out_shape=pltpu.VMEM((1, 1024), F32), in_specs=[hb...  30.5 us

profile of v4, /device:TPU:1, one launch (start us, length us, event | category | flops | bytes accessed | tf_op | source)
XLA Modules:
  0.0 31.8 jit_solution(14765834213690037982)
XLA Ops:
  0.6 0.0 copy-start
  0.6 0.0 copy-start.1
  0.7 30.5 %shard_map.104 = f32[1,1024]{1,0:T(1,128)S(1)} custom-call(f32[2]{0:T(128)} %angular_hbm.1, f32[36,1,1024]{2,1,0:T(1,128)} %bitcast.5, f32[36,1,1024]{2,1,0:T(1,128)} %bitcast.6, f32[1,1,1024]{2,1,0:T(1,128)} %bitcast.8, s32[6,1,1024]{2,1,0:T(1,128)} %bitcast.7, s32[1,1,1024]{2,1,0:T(1,128)} %bitcast.9, f32[2,2,1,1280]{3,2,1,0:T(1,128)} %source_hbm.1, ...), custom_call_target="tpu_custom_call" | custom-call | tf_op jit(solution)/shard_map/pallas_call | solution.py:462
  31.2 0.0 copy-done
  31.2 0.0 copy-done.1
  31.2 0.6 %exponential_multiply_fusion = (f32[1,1024]{1,0:T(1,128)}, f32[1,1024]{1,0:T(1,128)}) fusion(f32[1,1024]{1,0:T(1,128)S(1)} %copy-done, s32[1,1024]{1,0:T(1,128)S(1)} %copy-done.1, f32[1,1024]{1,0:T(1,128)S(1)} %shard_map.104), kind=kLoop, calls=%fused_computation | loop fusion | flops 5120 | bytes 20480 | tf_op jit(solution)/shard_map/mul | solution.py:514
Async XLA Ops:
  0.6 30.5 %copy-start = (f32[1,1024]{1,0:T(1,128)S(1)}, f32[1,1024]{1,0:T(1,128)}, u32[]{:S(2)}) copy-start(f32[1,1024]{1,0:T(1,128)} %param.12) | copy-start | bytes 12292
  0.6 30.5 %copy-start.1 = (s32[1,1024]{1,0:T(1,128)S(1)}, s32[1,1024]{1,0:T(1,128)}, u32[]{:S(2)}) copy-start(s32[1,1024]{1,0:T(1,128)} %param.14) | copy-start | bytes 12292

commit v5 on v4

--- a/solution.py
+++ b/solution.py
@@ -14,6 +14,7 @@
 EDGES = 1280
 CHUNKS = EDGES // 128
 GROUPS = 4
+WIDE = EDGES // RIM
 PARTS = 2
 STACK = 8 * PARTS
 HOPS = (0, 1, 2, 1)
@@ -75,6 +76,15 @@
         found = merged
         bit += 1
     return found[0]
+
+
+def pick_rims(low, high, index):
+    lane = index & 127
+    odd = (index & 128) != 0
+    wide = index >> 8
+    first = jnp.where(odd, lane_pick(low[:, 128:], lane), lane_pick(low[:, :128], lane))
+    last = jnp.where(odd, lane_pick(high[:, 128:], lane), lane_pick(high[:, :128], lane))
+    return jnp.where(wide == 0, first, jnp.where(wide == WIDE - 1, last, 0.0))
 
 
 def edge_dot(a, b, own=None):
@@ -110,7 +120,6 @@
     onehot,
     blocks,
     weight,
-    values,
     down_out,
     up_out,
     down_in,
@@ -223,16 +232,15 @@
         pl.when(me < DOM - 1)(copies[1].start)
         return copies
 
-    def join_rims(k, copies, field):
+    def take_rims(k, copies):
         pl.when(me < DOM - 1)(copies[0].wait_recv)
         pl.when(me > 0)(copies[1].wait_recv)
+        return permuted(up_in[k], order_rows), down_in[k]
+
+    def join(field, rims):
+        low, high = rims
         return jnp.concatenate(
-            [
-                field[:, :RIM] + permuted(up_in[k], order_rows),
-                field[:, RIM : EDGES - RIM],
-                field[:, EDGES - RIM :] + down_in[k],
-            ],
-            axis=1,
+            [field[:, :RIM] + low, field[:, RIM : EDGES - RIM], field[:, EDGES - RIM :] + high], axis=1
         )
 
     pl.semaphore_wait(barrier, len(NEAR) + 2 + end_pair.astype(jnp.int32) + start_pair.astype(jnp.int32))
@@ -293,43 +301,48 @@
     for d in (2, 6):
         signal(round_three, lax.rem(my_freq + d, FREQ), me)
 
-    def apply(field):
+    def apply(pick_all):
         out = None
         terms_of = []
         for q in range(GROUPS):
-            picked = [pick(field, ids[q, i]) for i in range(6)]
+            index = [ids[q, i] for i in range(6)]
+            picked = [pick_all(index[i]) for i in range(6)]
             term = weight[q, 0] * picked[0]
             for i in range(1, 6):
                 term = term + weight[q, i] * picked[i]
             terms_of.append(term)
+            columns = []
             for i in range(6):
                 running = blocks[q, 6 * i] * picked[0]
                 for j in range(1, 6):
                     running = running + blocks[q, 6 * i + j] * picked[j]
-                pieces = []
-                rest = running
-                for _ in range(PARTS - 1):
-                    head = rest.astype(BF16).astype(F32)
-                    pieces.append(head)
-                    rest = rest - head
-                pieces.append(rest)
-                stacked = jnp.concatenate(pieces, axis=0).astype(BF16)
-                for c in range(CHUNKS):
-                    values[q, STACK * c : STACK * (c + 1), 128 * i : 128 * (i + 1)] = (
-                        stacked * masks[q, c, :, 128 * i : 128 * (i + 1)]
+                head = running.astype(BF16).astype(F32)
+                stacked = jnp.concatenate([head, running - head], axis=0).astype(BF16)
+                columns.append(
+                    jnp.concatenate(
+                        [stacked * masks[q, c, :, 128 * i : 128 * (i + 1)] for c in range(CHUNKS)], axis=0
                     )
+                )
             product = lax.dot_general(
-                values[q], onehot[q], (((1,), (0,)), ((), ())), preferred_element_type=F32
+                jnp.concatenate(columns, axis=1),
+                onehot[q],
+                (((1,), (0,)), ((), ())),
+                preferred_element_type=F32,
             )
             out = product if out is None else out + product
         pieces = []
         for c in range(CHUNKS):
-            both = out[STACK * c : STACK * c + 8]
-            for s in range(1, PARTS):
-                both = both + out[STACK * c + 8 * s : STACK * c + 8 * s + 8]
+            both = out[STACK * c : STACK * c + 8] + out[STACK * c + 8 : STACK * c + 16]
             mixed = jnp.where(upper, both[:, :128], both[:, 128:])
             pieces.append(mixed + pltpu.roll(mixed, 4, 0))
         return jnp.concatenate(pieces, axis=1), jnp.concatenate(terms_of, axis=1)
+
+    def apply_own(field):
+        return apply(lambda index: pick(field, index))
+
+    def apply_rims(rims):
+        low, high = rims
+        return apply(lambda index: pick_rims(low, high, index))
 
     def send_sums(k, quantities):
         row = jnp.zeros((8, 128), F32)
@@ -358,39 +371,50 @@
 
     own = jnp.where(me > 0, 0.0, 1.0).astype(F32)
 
-    base = join_rims(0, rims0, sources)
-    image0, term0 = apply(base)
+    def finish(k, copies, own_part):
+        rims = take_rims(k, copies)
+        image, term = apply_rims(rims)
+        return rims, own_part[0] + image, own_part[1] + term
+
+    part = apply_own(sources)
+    rims, image0, term0 = finish(0, rims0, part)
     rims1 = send_rims(1, image0)
-    first = join_rims(1, rims1, image0)
+    base = join(sources, rims)
     pl.semaphore_wait(round_three, len(TWO_HOPS) + 2)
     send_sums(0, [edge_dot(base, base, own), edge_dot(base, image0)])
-    image1, term1 = apply(first)
+    part = apply_own(image0)
+    rims, image1, term1 = finish(1, rims1, part)
     rims2 = send_rims(2, image1)
-
-    second = join_rims(2, rims2, image1)
-    image2, term2 = apply(second)
+    first = join(image0, rims)
+    part = apply_own(image1)
 
     norm0, curve0 = take_sums(0, 2)
     alpha0 = norm0 / curve0
     residual = base - alpha0 * first
     residual_image = image0 - alpha0 * image1
+    early = [
+        edge_dot(residual, residual, own),
+        edge_dot(residual, residual_image),
+        edge_dot(base, residual_image),
+        edge_dot(first, first, own),
+        edge_dot(first, image1),
+    ]
+    near = term0 - alpha0 * term1
+
+    rims, image2, term2 = finish(2, rims2, part)
+    second = join(image1, rims)
     turned = first - alpha0 * second
     turned_image = image1 - alpha0 * image2
     send_sums(
         1,
-        [
-            edge_dot(residual, residual, own),
-            edge_dot(residual, residual_image),
-            edge_dot(base, residual_image),
-            edge_dot(first, first, own),
-            edge_dot(first, image1),
+        early
+        + [
             edge_dot(turned, turned, own),
             edge_dot(first, turned, own),
             edge_dot(turned, turned_image),
             edge_dot(first, turned_image),
         ],
     )
-    near = term0 - alpha0 * term1
     far = term1 - alpha0 * term2
 
     norm1, rr1, br1, bb2, bb3, rr2, br2, rr3, br3 = take_sums(1, 9)
@@ -479,7 +503,6 @@
             pltpu.VMEM((GROUPS, 768, 256), BF16),
             pltpu.VMEM((GROUPS, 36, 8, 128), F32),
             pltpu.VMEM((GROUPS, 6, 8, 128), F32),
-            pltpu.VMEM((GROUPS, STACK * CHUNKS, 768), BF16),
             pltpu.VMEM((3, 8, RIM), F32),
             pltpu.VMEM((3, 8, RIM), F32),
             pltpu.VMEM((3, 8, RIM), F32),

time: 31.9 us -> 31.5 us (0.987)
  Pallas kernels: 30.5 us -> 30.1 us
    pallas_call x1, Pallas kernels: 30.5 us -> 30.1 us  [local(): pl.pallas_call(kernel, out_shape=pltpu.VMEM((1, 1024), F32), in_specs=[hb...]
where the time goes in v5:
time: 31.5 us; the launch traced here: 31.4 us
  Pallas kernels  30.1 us (96%)
  between operations  0.67 us (2%)
  other arithmetic  0.62 us (2%)
    pallas_call x1, Pallas kernels, local(): pl.pallas_call(kernel, out_shape=pltpu.VMEM((1, 1024), F32), in_specs=[hb...  30.1 us

profile of v5, /device:TPU:1, one launch (start us, length us, event | category | flops | bytes accessed | tf_op | source)
XLA Modules:
  0.0 31.4 jit_solution(336766351454253474)
XLA Ops:
  0.6 0.0 copy-start
  0.6 0.0 copy-start.1
  0.7 30.1 %shard_map.104 = f32[1,1024]{1,0:T(1,128)S(1)} custom-call(f32[2]{0:T(128)} %angular_hbm.1, f32[36,1,1024]{2,1,0:T(1,128)} %bitcast.5, f32[36,1,1024]{2,1,0:T(1,128)} %bitcast.6, f32[1,1,1024]{2,1,0:T(1,128)} %bitcast.8, s32[6,1,1024]{2,1,0:T(1,128)} %bitcast.7, s32[1,1,1024]{2,1,0:T(1,128)} %bitcast.9, f32[2,2,1,1280]{3,2,1,0:T(1,128)} %source_hbm.1, ...), custom_call_target="tpu_custom_call" | custom-call | tf_op jit(solution)/shard_map/pallas_call | solution.py:486
  30.8 0.0 copy-done
  30.8 0.0 copy-done.1
  30.8 0.6 %exponential_multiply_fusion = (f32[1,1024]{1,0:T(1,128)}, f32[1,1024]{1,0:T(1,128)}) fusion(f32[1,1024]{1,0:T(1,128)S(1)} %copy-done, s32[1,1024]{1,0:T(1,128)S(1)} %copy-done.1, f32[1,1024]{1,0:T(1,128)S(1)} %shard_map.104), kind=kLoop, calls=%fused_computation | loop fusion | flops 5120 | bytes 20480 | tf_op jit(solution)/shard_map/mul | solution.py:537
Async XLA Ops:
  0.6 30.2 %copy-start = (f32[1,1024]{1,0:T(1,128)S(1)}, f32[1,1024]{1,0:T(1,128)}, u32[]{:S(2)}) copy-start(f32[1,1024]{1,0:T(1,128)} %param.12) | copy-start | bytes 12292
  0.6 30.2 %copy-start.1 = (s32[1,1024]{1,0:T(1,128)S(1)}, s32[1,1024]{1,0:T(1,128)}, u32[]{:S(2)}) copy-start(s32[1,1024]{1,0:T(1,128)} %param.14) | copy-start | bytes 12292

commit v6 on v4

--- a/solution.py
+++ b/solution.py
@@ -75,6 +75,12 @@
         found = merged
         bit += 1
     return found[0]
+
+
+def pick_rim(rim, index):
+    lane = index & 127
+    found = jnp.where((index & 128) != 0, lane_pick(rim[:, 128:], lane), lane_pick(rim[:, :128], lane))
+    return jnp.where(index < RIM, found, jnp.zeros_like(found))
 
 
 def edge_dot(a, b, own=None):
@@ -106,22 +112,20 @@
     forward,
     order,
     ids,
+    late_ids,
     masks,
     onehot,
     blocks,
     weight,
-    values,
     down_out,
     up_out,
-    down_in,
-    up_in,
+    rim_in,
     sums,
     terms,
     load_sem,
     down_send,
-    down_recv,
     up_send,
-    up_recv,
+    rim_recv,
     sum_send,
     sum_recv,
     term_send,
@@ -190,13 +194,15 @@
     ).astype(jnp.int32)
     sources = field_rows(source)
 
-    @pl.when(me == 0)
+    even = lax.rem(me, 2) == 0
+    late_side = lax.rem(me, 2)
+    early_side = 1 - late_side
+    has_late = (me > 0) & (me < DOM - 1)
+
+    @pl.when(jnp.logical_not(has_late))
     def _():
-        up_in[...] = jnp.zeros((3, 8, RIM), F32)
-
-    @pl.when(me == DOM - 1)
-    def _():
-        down_in[...] = jnp.zeros((3, 8, RIM), F32)
+        for k in range(3):
+            rim_in[k, late_side] = jnp.zeros((8, RIM), F32)
 
     def send_rims(k, field):
         down_out[k] = permuted(field[:, :RIM], inverse)
@@ -204,17 +210,17 @@
         copies = (
             pltpu.make_async_remote_copy(
                 src_ref=down_out.at[k],
-                dst_ref=down_in.at[k],
+                dst_ref=rim_in.at[k, 1],
                 send_sem=down_send.at[k],
-                recv_sem=down_recv.at[k],
+                recv_sem=rim_recv.at[k, 1],
                 device_id=(my_freq, below),
                 device_id_type=MESH,
             ),
             pltpu.make_async_remote_copy(
                 src_ref=up_out.at[k],
-                dst_ref=up_in.at[k],
+                dst_ref=rim_in.at[k, 0],
                 send_sem=up_send.at[k],
-                recv_sem=up_recv.at[k],
+                recv_sem=rim_recv.at[k, 0],
                 device_id=(my_freq, above),
                 device_id_type=MESH,
             ),
@@ -223,14 +229,17 @@
         pl.when(me < DOM - 1)(copies[1].start)
         return copies
 
-    def join_rims(k, copies, field):
-        pl.when(me < DOM - 1)(copies[0].wait_recv)
-        pl.when(me > 0)(copies[1].wait_recv)
+    def take_rim(k, side):
+        rim = rim_in.at[k, side]
+        return pltpu.make_async_copy(rim, rim, rim_recv.at[k, side]).wait
+
+    def join(field, rim, low_side):
+        zero = jnp.zeros((8, RIM), F32)
         return jnp.concatenate(
             [
-                field[:, :RIM] + permuted(up_in[k], order_rows),
+                field[:, :RIM] + jnp.where(low_side, permuted(rim, order_rows), zero),
                 field[:, RIM : EDGES - RIM],
-                field[:, EDGES - RIM :] + down_in[k],
+                field[:, EDGES - RIM :] + jnp.where(low_side, zero, rim),
             ],
             axis=1,
         )
@@ -248,6 +257,8 @@
         for i in range(6):
             index = halves(edges, i, q)
             ids[q, i] = index
+            mapped = pick_rim(order_rows, index)
+            late_ids[q, i] = jnp.where(even, jnp.where(index < RIM, mapped, RIM), jnp.where(index >= EDGES - RIM, index - (EDGES - RIM), RIM))
             wide = index >> 7
             for c in range(CHUNKS):
                 hit = jnp.where(wide == c, 1.0, 0.0)
@@ -293,50 +304,61 @@
     for d in (2, 6):
         signal(round_three, lax.rem(my_freq + d, FREQ), me)
 
-    def apply(field):
+    def apply(pick_all):
         out = None
         terms_of = []
         for q in range(GROUPS):
-            picked = [pick(field, ids[q, i]) for i in range(6)]
+            picked = [pick_all(q, i) for i in range(6)]
             term = weight[q, 0] * picked[0]
             for i in range(1, 6):
                 term = term + weight[q, i] * picked[i]
             terms_of.append(term)
+            columns = []
             for i in range(6):
                 running = blocks[q, 6 * i] * picked[0]
                 for j in range(1, 6):
                     running = running + blocks[q, 6 * i + j] * picked[j]
-                pieces = []
-                rest = running
-                for _ in range(PARTS - 1):
-                    head = rest.astype(BF16).astype(F32)
-                    pieces.append(head)
-                    rest = rest - head
-                pieces.append(rest)
-                stacked = jnp.concatenate(pieces, axis=0).astype(BF16)
-                for c in range(CHUNKS):
-                    values[q, STACK * c : STACK * (c + 1), 128 * i : 128 * (i + 1)] = (
-                        stacked * masks[q, c, :, 128 * i : 128 * (i + 1)]
+                head = running.astype(BF16).astype(F32)
+                stacked = jnp.concatenate([head, running - head], axis=0).astype(BF16)
+                columns.append(
+                    jnp.concatenate(
+                        [stacked * masks[q, c, :, 128 * i : 128 * (i + 1)] for c in range(CHUNKS)], axis=0
                     )
+                )
             product = lax.dot_general(
-                values[q], onehot[q], (((1,), (0,)), ((), ())), preferred_element_type=F32
+                jnp.concatenate(columns, axis=1),
+                onehot[q],
+                (((1,), (0,)), ((), ())),
+                preferred_element_type=F32,
             )
             out = product if out is None else out + product
         pieces = []
         for c in range(CHUNKS):
-            both = out[STACK * c : STACK * c + 8]
-            for s in range(1, PARTS):
-                both = both + out[STACK * c + 8 * s : STACK * c + 8 * s + 8]
+            both = out[STACK * c : STACK * c + 8] + out[STACK * c + 8 : STACK * c + 16]
             mixed = jnp.where(upper, both[:, :128], both[:, 128:])
             pieces.append(mixed + pltpu.roll(mixed, 4, 0))
         return jnp.concatenate(pieces, axis=1), jnp.concatenate(terms_of, axis=1)
 
-    def send_sums(k, quantities):
+    def apply_early(k, field):
+        take_rim(k, early_side)()
+        joined = join(field, rim_in[k, early_side], jnp.logical_not(even))
+        return joined, apply(lambda q, i: pick(joined, ids[q, i]))
+
+    def apply_late(k, part):
+        pl.when(has_late)(take_rim(k, late_side))
+        rim = rim_in[k, late_side]
+        image, term = apply(lambda q, i: pick_rim(rim, late_ids[q, i]))
+        return rim, part[0] + image, part[1] + term
+
+    def pack_sums(start, quantities):
         row = jnp.zeros((8, 128), F32)
-        for n, quantity in enumerate(quantities):
+        for n, quantity in enumerate(quantities, start):
             column = jnp.sum(quantity, axis=1, keepdims=True)
             row = row + jnp.where((lane == 4 * n + sub) & upper, column, 0.0)
-        sums[k, me] = jnp.sum(row, axis=0, keepdims=True)
+        return jnp.sum(row, axis=0, keepdims=True)
+
+    def send_sums(k, row):
+        sums[k, me] = row
         for n in DOM_PEERS:
             pltpu.make_async_remote_copy(
                 src_ref=sums.at[k, me],
@@ -358,39 +380,48 @@
 
     own = jnp.where(me > 0, 0.0, 1.0).astype(F32)
 
-    base = join_rims(0, rims0, sources)
-    image0, term0 = apply(base)
+    base, part = apply_early(0, sources)
+    rim, image0, term0 = apply_late(0, part)
     rims1 = send_rims(1, image0)
-    first = join_rims(1, rims1, image0)
+    base = join(base, rim, even)
     pl.semaphore_wait(round_three, len(TWO_HOPS) + 2)
-    send_sums(0, [edge_dot(base, base, own), edge_dot(base, image0)])
-    image1, term1 = apply(first)
+    send_sums(0, pack_sums(0, [edge_dot(base, base, own), edge_dot(base, image0)]))
+    first, part = apply_early(1, image0)
+    rim, image1, term1 = apply_late(1, part)
     rims2 = send_rims(2, image1)
-
-    second = join_rims(2, rims2, image1)
-    image2, term2 = apply(second)
+    first = join(first, rim, even)
+    second, part = apply_early(2, image1)
 
     norm0, curve0 = take_sums(0, 2)
     alpha0 = norm0 / curve0
     residual = base - alpha0 * first
     residual_image = image0 - alpha0 * image1
-    turned = first - alpha0 * second
-    turned_image = image1 - alpha0 * image2
-    send_sums(
-        1,
+    early_sums = pack_sums(
+        0,
         [
             edge_dot(residual, residual, own),
             edge_dot(residual, residual_image),
             edge_dot(base, residual_image),
             edge_dot(first, first, own),
             edge_dot(first, image1),
+        ],
+    )
+    near = term0 - alpha0 * term1
+
+    rim, image2, term2 = apply_late(2, part)
+    second = join(second, rim, even)
+    turned = first - alpha0 * second
+    turned_image = image1 - alpha0 * image2
+    late_sums = pack_sums(
+        5,
+        [
             edge_dot(turned, turned, own),
             edge_dot(first, turned, own),
             edge_dot(turned, turned_image),
             edge_dot(first, turned_image),
         ],
     )
-    near = term0 - alpha0 * term1
+    send_sums(1, early_sums + late_sums)
     far = term1 - alpha0 * term2
 
     norm1, rr1, br1, bb2, bb3, rr2, br2, rr3, br3 = take_sums(1, 9)
@@ -475,22 +506,20 @@
             pltpu.VMEM((2, 2, 1, EDGES), F32),
             pltpu.VMEM((1, RIM), jnp.int32),
             pltpu.VMEM((GROUPS, 6, 8, 128), jnp.int32),
+            pltpu.VMEM((GROUPS, 6, 8, 128), jnp.int32),
             pltpu.VMEM((GROUPS, CHUNKS, STACK, 768), BF16),
             pltpu.VMEM((GROUPS, 768, 256), BF16),
             pltpu.VMEM((GROUPS, 36, 8, 128), F32),
             pltpu.VMEM((GROUPS, 6, 8, 128), F32),
-            pltpu.VMEM((GROUPS, STACK * CHUNKS, 768), BF16),
             pltpu.VMEM((3, 8, RIM), F32),
             pltpu.VMEM((3, 8, RIM), F32),
-            pltpu.VMEM((3, 8, RIM), F32),
-            pltpu.VMEM((3, 8, RIM), F32),
+            pltpu.VMEM((3, 2, 8, RIM), F32),
             pltpu.VMEM((2, DOM, 1, 128), F32),
             pltpu.VMEM((FREQ, 8, 128), F32),
             dma((9,)),
             dma((3,)),
             dma((3,)),
-            dma((3,)),
-            dma((3,)),
+            dma((3, 2)),
             dma((3,)),
             dma((3,)),
             dma,

time: 31.9 us -> 31.2 us (0.978)
  Pallas kernels: 30.5 us -> 29.9 us
    pallas_call x1, Pallas kernels: 30.5 us -> 29.9 us  [local(): pl.pallas_call(kernel, out_shape=pltpu.VMEM((1, 1024), F32), in_specs=[hb...]
where the time goes in v6:
time: 31.2 us; the launch traced here: 31.1 us
  Pallas kernels  29.9 us (96%)
  between operations  0.67 us (2%)
  other arithmetic  0.62 us (2%)
    pallas_call x1, Pallas kernels, local(): pl.pallas_call(kernel, out_shape=pltpu.VMEM((1, 1024), F32), in_specs=[hb...  29.9 us

profile of v6, /device:TPU:1, one launch (start us, length us, event | category | flops | bytes accessed | tf_op | source)
XLA Modules:
  0.0 31.1 jit_solution(6171344348911211999)
XLA Ops:
  0.6 0.0 copy-start
  0.6 0.0 copy-start.1
  0.7 29.9 %shard_map.104 = f32[1,1024]{1,0:T(1,128)S(1)} custom-call(f32[2]{0:T(128)} %angular_hbm.1, f32[36,1,1024]{2,1,0:T(1,128)} %bitcast.5, f32[36,1,1024]{2,1,0:T(1,128)} %bitcast.6, f32[1,1,1024]{2,1,0:T(1,128)} %bitcast.8, s32[6,1,1024]{2,1,0:T(1,128)} %bitcast.7, s32[1,1,1024]{2,1,0:T(1,128)} %bitcast.9, f32[2,2,1,1280]{3,2,1,0:T(1,128)} %source_hbm.1, ...), custom_call_target="tpu_custom_call" | custom-call | tf_op jit(solution)/shard_map/pallas_call | solution.py:493
  30.5 0.0 copy-done
  30.5 0.0 copy-done.1
  30.5 0.6 %exponential_multiply_fusion = (f32[1,1024]{1,0:T(1,128)}, f32[1,1024]{1,0:T(1,128)}) fusion(f32[1,1024]{1,0:T(1,128)S(1)} %copy-done, s32[1,1024]{1,0:T(1,128)S(1)} %copy-done.1, f32[1,1024]{1,0:T(1,128)S(1)} %shard_map.104), kind=kLoop, calls=%fused_computation | loop fusion | flops 5120 | bytes 20480 | tf_op jit(solution)/shard_map/mul | solution.py:543
Async XLA Ops:
  0.6 29.9 %copy-start = (f32[1,1024]{1,0:T(1,128)S(1)}, f32[1,1024]{1,0:T(1,128)}, u32[]{:S(2)}) copy-start(f32[1,1024]{1,0:T(1,128)} %param.12) | copy-start | bytes 12292
  0.6 29.9 %copy-start.1 = (s32[1,1024]{1,0:T(1,128)S(1)}, s32[1,1024]{1,0:T(1,128)}, u32[]{:S(2)}) copy-start(s32[1,1024]{1,0:T(1,128)} %param.14) | copy-start | bytes 12292

commit v7 on v6

--- a/solution.py
+++ b/solution.py
@@ -117,6 +117,8 @@
     onehot,
     blocks,
     weight,
+    kept,
+    kept_next,
     down_out,
     up_out,
     rim_in,
@@ -205,7 +207,6 @@
             rim_in[k, late_side] = jnp.zeros((8, RIM), F32)
 
     def send_rims(k, field):
-        down_out[k] = permuted(field[:, :RIM], inverse)
         up_out[k] = field[:, EDGES - RIM :]
         copies = (
             pltpu.make_async_remote_copy(
@@ -225,8 +226,9 @@
                 device_id_type=MESH,
             ),
         )
+        pl.when(me < DOM - 1)(copies[1].start)
+        down_out[k] = permuted(field[:, :RIM], inverse)
         pl.when(me > 0)(copies[0].start)
-        pl.when(me < DOM - 1)(copies[1].start)
         return copies
 
     def take_rim(k, side):
@@ -304,11 +306,14 @@
     for d in (2, 6):
         signal(round_three, lax.rem(my_freq + d, FREQ), me)
 
-    def apply(pick_all):
+    def apply(pick_all, keep=None):
         out = None
         terms_of = []
         for q in range(GROUPS):
             picked = [pick_all(q, i) for i in range(6)]
+            if keep is not None:
+                for i in range(6):
+                    kept[q, i] = picked[i] if keep == 0 else kept[q, i] + picked[i]
             term = weight[q, 0] * picked[0]
             for i in range(1, 6):
                 term = term + weight[q, i] * picked[i]
@@ -339,15 +344,21 @@
             pieces.append(mixed + pltpu.roll(mixed, 4, 0))
         return jnp.concatenate(pieces, axis=1), jnp.concatenate(terms_of, axis=1)
 
+    def join_early(k, field):
+        take_rim(k, early_side)()
+        return join(field, rim_in[k, early_side], jnp.logical_not(even))
+
+    def late_rim(k):
+        pl.when(has_late)(take_rim(k, late_side))
+        return rim_in[k, late_side]
+
     def apply_early(k, field):
-        take_rim(k, early_side)()
-        joined = join(field, rim_in[k, early_side], jnp.logical_not(even))
-        return joined, apply(lambda q, i: pick(joined, ids[q, i]))
+        joined = join_early(k, field)
+        return joined, apply(lambda q, i: pick(joined, ids[q, i]), keep=0 if k == 1 else None)
 
     def apply_late(k, part):
-        pl.when(has_late)(take_rim(k, late_side))
-        rim = rim_in[k, late_side]
-        image, term = apply(lambda q, i: pick_rim(rim, late_ids[q, i]))
+        rim = late_rim(k)
+        image, term = apply(lambda q, i: pick_rim(rim, late_ids[q, i]), keep=1 if k == 1 else None)
         return rim, part[0] + image, part[1] + term
 
     def pack_sums(start, quantities):
@@ -390,7 +401,10 @@
     rim, image1, term1 = apply_late(1, part)
     rims2 = send_rims(2, image1)
     first = join(first, rim, even)
-    second, part = apply_early(2, image1)
+    second = join_early(2, image1)
+    for q in range(GROUPS):
+        for i in range(6):
+            kept_next[q, i] = pick(second, ids[q, i])
 
     norm0, curve0 = take_sums(0, 2)
     alpha0 = norm0 / curve0
@@ -407,22 +421,38 @@
         ],
     )
     near = term0 - alpha0 * term1
-
-    rim, image2, term2 = apply_late(2, part)
-    second = join(second, rim, even)
-    turned = first - alpha0 * second
-    turned_image = image1 - alpha0 * image2
+    for q in range(GROUPS):
+        for i in range(6):
+            kept[q, i] = kept[q, i] - alpha0 * kept_next[q, i]
+
+    rim = late_rim(2)
+    energy = None
+    far = []
+    for q in range(GROUPS):
+        picked = [kept[q, i] - alpha0 * pick_rim(rim, late_ids[q, i]) for i in range(6)]
+        term = weight[q, 0] * picked[0]
+        for i in range(1, 6):
+            term = term + weight[q, i] * picked[i]
+        far.append(term)
+        for i in range(6):
+            running = 0.5 * (blocks[q, 7 * i] * picked[i])
+            for j in range(i + 1, 6):
+                running = running + blocks[q, 6 * i + j] * picked[j]
+            product = picked[i] * running
+            energy = product if energy is None else energy + product
+    far = jnp.concatenate(far, axis=1)
+    energy = 2.0 * (energy + pltpu.roll(energy, 4, 0))
+    turned = first - alpha0 * join(second, rim, even)
     late_sums = pack_sums(
         5,
         [
             edge_dot(turned, turned, own),
             edge_dot(first, turned, own),
-            edge_dot(turned, turned_image),
-            edge_dot(first, turned_image),
+            energy,
+            edge_dot(image1, turned),
         ],
     )
     send_sums(1, early_sums + late_sums)
-    far = term1 - alpha0 * term2
 
     norm1, rr1, br1, bb2, bb3, rr2, br2, rr3, br3 = take_sums(1, 9)
     beta0 = norm1 / norm0
@@ -511,6 +541,8 @@
             pltpu.VMEM((GROUPS, 768, 256), BF16),
             pltpu.VMEM((GROUPS, 36, 8, 128), F32),
             pltpu.VMEM((GROUPS, 6, 8, 128), F32),
+            pltpu.VMEM((GROUPS, 6, 8, 128), F32),
+            pltpu.VMEM((GROUPS, 6, 8, 128), F32),
             pltpu.VMEM((3, 8, RIM), F32),
             pltpu.VMEM((3, 8, RIM), F32),
             pltpu.VMEM((3, 2, 8, RIM), F32),

time: 31.2 us -> 30.7 us (0.984)
  Pallas kernels: 29.9 us -> 29.3 us
    pallas_call x1, Pallas kernels: 29.9 us -> 29.3 us  [local(): pl.pallas_call(kernel, out_shape=pltpu.VMEM((1, 1024), F32), in_specs=[hb...]
where the time goes in v7:
time: 30.7 us; the launch traced here: 30.6 us
  Pallas kernels  29.3 us (95%)
  between operations  0.67 us (2%)
  other arithmetic  0.62 us (2%)
    pallas_call x1, Pallas kernels, local(): pl.pallas_call(kernel, out_shape=pltpu.VMEM((1, 1024), F32), in_specs=[hb...  29.3 us
    mul x1, other arithmetic, local(): updated = conductivity * jnp.exp(-0.5 * jnp.tanh(gradient))  0.62 us

profile of v7, /device:TPU:1, one launch (start us, length us, event | category | flops | bytes accessed | tf_op | source)
XLA Modules:
  0.0 30.6 jit_solution(3339138384330554424)
XLA Ops:
  0.6 0.0 copy-start
  0.6 0.0 copy-start.1
  0.7 29.3 %shard_map.104 = f32[1,1024]{1,0:T(1,128)S(1)} custom-call(f32[2]{0:T(128)} %angular_hbm.1, f32[36,1,1024]{2,1,0:T(1,128)} %bitcast.5, f32[36,1,1024]{2,1,0:T(1,128)} %bitcast.6, f32[1,1,1024]{2,1,0:T(1,128)} %bitcast.8, s32[6,1,1024]{2,1,0:T(1,128)} %bitcast.7, s32[1,1,1024]{2,1,0:T(1,128)} %bitcast.9, f32[2,2,1,1280]{3,2,1,0:T(1,128)} %source_hbm.1, ...), custom_call_target="tpu_custom_call" | custom-call | tf_op jit(solution)/shard_map/pallas_call | solution.py:523
  30.0 0.0 copy-done
  30.0 0.0 copy-done.1
  30.0 0.6 %exponential_multiply_fusion = (f32[1,1024]{1,0:T(1,128)}, f32[1,1024]{1,0:T(1,128)}) fusion(f32[1,1024]{1,0:T(1,128)S(1)} %copy-done, s32[1,1024]{1,0:T(1,128)S(1)} %copy-done.1, f32[1,1024]{1,0:T(1,128)S(1)} %shard_map.104), kind=kLoop, calls=%fused_computation | loop fusion | flops 5120 | bytes 20480 | tf_op jit(solution)/shard_map/mul | solution.py:575
Async XLA Ops:
  0.6 29.4 %copy-start = (f32[1,1024]{1,0:T(1,128)S(1)}, f32[1,1024]{1,0:T(1,128)}, u32[]{:S(2)}) copy-start(f32[1,1024]{1,0:T(1,128)} %param.12) | copy-start | bytes 12292
  0.6 29.4 %copy-start.1 = (s32[1,1024]{1,0:T(1,128)S(1)}, s32[1,1024]{1,0:T(1,128)}, u32[]{:S(2)}) copy-start(s32[1,1024]{1,0:T(1,128)} %param.14) | copy-start | bytes 12292

commit v8 on v7

--- a/solution.py
+++ b/solution.py
@@ -14,6 +14,7 @@
 EDGES = 1280
 CHUNKS = EDGES // 128
 GROUPS = 4
+AHEAD = 2
 PARTS = 2
 STACK = 8 * PARTS
 HOPS = (0, 1, 2, 1)
@@ -115,18 +116,18 @@
     late_ids,
     masks,
     onehot,
+    late_masks,
+    late_hot,
     blocks,
     weight,
     kept,
     kept_next,
-    down_out,
-    up_out,
+    rim_out,
     rim_in,
     sums,
     terms,
     load_sem,
-    down_send,
-    up_send,
+    rim_send,
     rim_recv,
     sum_send,
     sum_recv,
@@ -206,34 +207,40 @@
         for k in range(3):
             rim_in[k, late_side] = jnp.zeros((8, RIM), F32)
 
-    def send_rims(k, field):
-        up_out[k] = field[:, EDGES - RIM :]
-        copies = (
-            pltpu.make_async_remote_copy(
-                src_ref=down_out.at[k],
-                dst_ref=rim_in.at[k, 1],
-                send_sem=down_send.at[k],
-                recv_sem=rim_recv.at[k, 1],
-                device_id=(my_freq, below),
-                device_id_type=MESH,
-            ),
-            pltpu.make_async_remote_copy(
-                src_ref=up_out.at[k],
-                dst_ref=rim_in.at[k, 0],
-                send_sem=up_send.at[k],
-                recv_sem=rim_recv.at[k, 0],
-                device_id=(my_freq, above),
-                device_id_type=MESH,
-            ),
+    late_peer = jnp.where(even, below, above)
+
+    def rim_copy(k, n):
+        side, peer = ((early_side, late_peer), (late_side, me ^ 1))[n]
+        return pltpu.make_async_remote_copy(
+            src_ref=rim_out.at[k, n, pl.ds(0, 4)],
+            dst_ref=rim_in.at[k, side, pl.ds(0, 4)],
+            send_sem=rim_send.at[k, n],
+            recv_sem=rim_recv.at[k, side],
+            device_id=(my_freq, peer),
+            device_id_type=MESH,
         )
-        pl.when(me < DOM - 1)(copies[1].start)
-        down_out[k] = permuted(field[:, :RIM], inverse)
-        pl.when(me > 0)(copies[0].start)
-        return copies
+
+    def send_late(k, rim):
+        rim_out[k, 0] = jnp.where(even, permuted(rim, inverse), rim)
+        pl.when(has_late)(rim_copy(k, 0).start)
+
+    def send_early(k, rim):
+        rim_out[k, 1] = jnp.where(even, rim, permuted(rim, inverse))
+        rim_copy(k, 1).start()
+
+    def late_part(field):
+        return jnp.where(even, field[:, :RIM], field[:, EDGES - RIM :])
+
+    def early_part(field):
+        return jnp.where(even, field[:, EDGES - RIM :], field[:, :RIM])
 
     def take_rim(k, side):
-        rim = rim_in.at[k, side]
+        rim = rim_in.at[k, side, pl.ds(0, 4)]
         return pltpu.make_async_copy(rim, rim, rim_recv.at[k, side]).wait
+
+    def received(k, side):
+        rim = rim_in[k, side, pl.ds(0, 4)]
+        return jnp.concatenate([rim, rim], axis=0)
 
     def join(field, rim, low_side):
         zero = jnp.zeros((8, RIM), F32)
@@ -246,13 +253,6 @@
             axis=1,
         )
 
-    pl.semaphore_wait(barrier, len(NEAR) + 2 + end_pair.astype(jnp.int32) + start_pair.astype(jnp.int32))
-    rims0 = send_rims(0, sources)
-    for k in ONE_HOP:
-        signal(round_two, my_freq, me ^ k)
-    for d in (1, 7):
-        signal(round_two, lax.rem(my_freq + d, FREQ), me)
-
     loads[2].wait()
 
     def tables(q, carry):
@@ -260,23 +260,45 @@
             index = halves(edges, i, q)
             ids[q, i] = index
             mapped = pick_rim(order_rows, index)
+            in_late = jnp.where(even, index, index - (EDGES - RIM))
+            quarter = jnp.where((in_late >= 0) & (in_late < RIM), in_late >> 6, 4)
+            for c in range(4):
+                hit = jnp.where(quarter == c, 1.0, 0.0)
+                late_masks[q, c, :, 128 * i : 128 * (i + 1)] = jnp.concatenate([hit] * PARTS, axis=0).astype(BF16)
             late_ids[q, i] = jnp.where(even, jnp.where(index < RIM, mapped, RIM), jnp.where(index >= EDGES - RIM, index - (EDGES - RIM), RIM))
             wide = index >> 7
             for c in range(CHUNKS):
                 hit = jnp.where(wide == c, 1.0, 0.0)
                 masks[q, c, :, 128 * i : 128 * (i + 1)] = jnp.concatenate([hit] * PARTS, axis=0).astype(BF16)
+        columns = []
         for h in range(2):
             at = pl.ds(pl.multiple_of(512 * h + 128 * q, 128), 128)
             stacked = spread(edges[0, :, at])
             for i in range(1, 6):
                 stacked = jnp.where(sub == i, spread(edges[i, :, at]), stacked)
-            columns = jnp.transpose(stacked & 127)
-            for i in range(6):
-                hit = jnp.broadcast_to(columns[:, i : i + 1], (128, 128)) == lanes_iota((128, 128))
-                onehot[q, 128 * i : 128 * (i + 1), 128 * h : 128 * (h + 1)] = jnp.where(hit, 1.0, 0.0).astype(BF16)
+            columns.append(jnp.transpose(stacked & 127))
+        across = lanes_iota((128, 128))
+        for i in range(6):
+            wide = [jnp.broadcast_to(columns[h][:, i : i + 1], (128, 128)) for h in range(2)]
+            for h in range(2):
+                onehot[q, 128 * i : 128 * (i + 1), 128 * h : 128 * (h + 1)] = jnp.where(
+                    wide[h] == across, 1.0, 0.0
+                ).astype(BF16)
+            short = jnp.where(across < 64, wide[0] & 63, (wide[1] & 63) + 64)
+            late_hot[q, 128 * i : 128 * (i + 1)] = jnp.where(short == across, 1.0, 0.0).astype(BF16)
         return carry
 
-    lax.fori_loop(0, GROUPS, tables, 0)
+    lax.fori_loop(0, AHEAD, tables, 0)
+
+    pl.semaphore_wait(barrier, len(NEAR) + 2 + end_pair.astype(jnp.int32) + start_pair.astype(jnp.int32))
+    send_late(0, late_part(sources))
+    send_early(0, early_part(sources))
+    for k in ONE_HOP:
+        signal(round_two, my_freq, me ^ k)
+    for d in (1, 7):
+        signal(round_two, lax.rem(my_freq + d, FREQ), me)
+
+    lax.fori_loop(AHEAD, GROUPS, tables, 0)
 
     for n in range(3, 9):
         loads[n].wait()
@@ -306,9 +328,9 @@
     for d in (2, 6):
         signal(round_three, lax.rem(my_freq + d, FREQ), me)
 
-    def apply(pick_all, keep=None):
-        out = None
+    def element_values(pick_all, keep=None):
         terms_of = []
+        values = []
         for q in range(GROUPS):
             picked = [pick_all(q, i) for i in range(6)]
             if keep is not None:
@@ -318,48 +340,67 @@
             for i in range(1, 6):
                 term = term + weight[q, i] * picked[i]
             terms_of.append(term)
-            columns = []
             for i in range(6):
                 running = blocks[q, 6 * i] * picked[0]
                 for j in range(1, 6):
                     running = running + blocks[q, 6 * i + j] * picked[j]
                 head = running.astype(BF16).astype(F32)
-                stacked = jnp.concatenate([head, running - head], axis=0).astype(BF16)
-                columns.append(
-                    jnp.concatenate(
-                        [stacked * masks[q, c, :, 128 * i : 128 * (i + 1)] for c in range(CHUNKS)], axis=0
-                    )
+                values.append(jnp.concatenate([head, running - head], axis=0).astype(BF16))
+        return values, jnp.concatenate(terms_of, axis=1)
+
+    def add_up(values, chosen, table, count):
+        out = None
+        for q in range(GROUPS):
+            columns = [
+                jnp.concatenate(
+                    [values[6 * q + i] * chosen[q, c, :, 128 * i : 128 * (i + 1)] for c in range(count)], axis=0
                 )
+                for i in range(6)
+            ]
             product = lax.dot_general(
-                jnp.concatenate(columns, axis=1),
-                onehot[q],
-                (((1,), (0,)), ((), ())),
-                preferred_element_type=F32,
+                jnp.concatenate(columns, axis=1), table[q], (((1,), (0,)), ((), ())), preferred_element_type=F32
             )
             out = product if out is None else out + product
+        return [out[STACK * c : STACK * c + 8] + out[STACK * c + 8 : STACK * c + 16] for c in range(count)]
+
+    def scatter(values):
         pieces = []
-        for c in range(CHUNKS):
-            both = out[STACK * c : STACK * c + 8] + out[STACK * c + 8 : STACK * c + 16]
+        for both in add_up(values, masks, onehot, CHUNKS):
             mixed = jnp.where(upper, both[:, :128], both[:, 128:])
             pieces.append(mixed + pltpu.roll(mixed, 4, 0))
-        return jnp.concatenate(pieces, axis=1), jnp.concatenate(terms_of, axis=1)
+        return jnp.concatenate(pieces, axis=1)
+
+    def scatter_late(values):
+        found = add_up(values, late_masks, late_hot, 4)
+        turned_lanes = [pltpu.roll(both, 64, 1) for both in found]
+        pieces = []
+        for c in (0, 2):
+            left = jnp.where(upper, found[c], turned_lanes[c])
+            right = jnp.where(upper, turned_lanes[c + 1], found[c + 1])
+            mixed = jnp.where(lane < 64, left, right)
+            pieces.append(mixed + pltpu.roll(mixed, 4, 0))
+        return jnp.concatenate(pieces, axis=1)
 
     def join_early(k, field):
         take_rim(k, early_side)()
-        return join(field, rim_in[k, early_side], jnp.logical_not(even))
+        return join(field, received(k, early_side), jnp.logical_not(even))
 
     def late_rim(k):
         pl.when(has_late)(take_rim(k, late_side))
-        return rim_in[k, late_side]
+        return received(k, late_side)
 
     def apply_early(k, field):
         joined = join_early(k, field)
-        return joined, apply(lambda q, i: pick(joined, ids[q, i]), keep=0 if k == 1 else None)
+        values, term = element_values(lambda q, i: pick(joined, ids[q, i]), keep=0 if k == 1 else None)
+        return joined, (scatter(values), term)
 
     def apply_late(k, part):
         rim = late_rim(k)
-        image, term = apply(lambda q, i: pick_rim(rim, late_ids[q, i]), keep=1 if k == 1 else None)
-        return rim, part[0] + image, part[1] + term
+        values, term = element_values(lambda q, i: pick_rim(rim, late_ids[q, i]), keep=1 if k == 1 else None)
+        send_late(k + 1, late_part(part[0]) + scatter_late(values))
+        image = part[0] + scatter(values)
+        send_early(k + 1, early_part(image))
+        return rim, image, part[1] + term
 
     def pack_sums(start, quantities):
         row = jnp.zeros((8, 128), F32)
@@ -393,13 +434,11 @@
 
     base, part = apply_early(0, sources)
     rim, image0, term0 = apply_late(0, part)
-    rims1 = send_rims(1, image0)
     base = join(base, rim, even)
     pl.semaphore_wait(round_three, len(TWO_HOPS) + 2)
     send_sums(0, pack_sums(0, [edge_dot(base, base, own), edge_dot(base, image0)]))
     first, part = apply_early(1, image0)
     rim, image1, term1 = apply_late(1, part)
-    rims2 = send_rims(2, image1)
     first = join(first, rim, even)
     second = join_early(2, image1)
     for q in range(GROUPS):
@@ -491,9 +530,9 @@
             device_id=(peer, me),
             device_id_type=MESH,
         ).start()
-    for copies in (rims0, rims1, rims2):
-        pl.when(me > 0)(copies[0].wait_send)
-        pl.when(me < DOM - 1)(copies[1].wait_send)
+    for k in range(3):
+        pl.when(has_late)(rim_copy(k, 0).wait_send)
+        rim_copy(k, 1).wait_send()
     for k in range(2):
         sent = sums.at[k, pl.ds(0, DOM - 1)]
         pltpu.make_async_copy(sent, sent, sum_send.at[k]).wait()
@@ -539,18 +578,18 @@
             pltpu.VMEM((GROUPS, 6, 8, 128), jnp.int32),
             pltpu.VMEM((GROUPS, CHUNKS, STACK, 768), BF16),
             pltpu.VMEM((GROUPS, 768, 256), BF16),
+            pltpu.VMEM((GROUPS, 4, STACK, 768), BF16),
+            pltpu.VMEM((GROUPS, 768, 128), BF16),
             pltpu.VMEM((GROUPS, 36, 8, 128), F32),
             pltpu.VMEM((GROUPS, 6, 8, 128), F32),
             pltpu.VMEM((GROUPS, 6, 8, 128), F32),
             pltpu.VMEM((GROUPS, 6, 8, 128), F32),
-            pltpu.VMEM((3, 8, RIM), F32),
-            pltpu.VMEM((3, 8, RIM), F32),
+            pltpu.VMEM((3, 2, 8, RIM), F32),
             pltpu.VMEM((3, 2, 8, RIM), F32),
             pltpu.VMEM((2, DOM, 1, 128), F32),
             pltpu.VMEM((FREQ, 8, 128), F32),
             dma((9,)),
-            dma((3,)),
-            dma((3,)),
+            dma((3, 2)),
             dma((3, 2)),
             dma((3,)),
             dma((3,)),

time: 30.7 us -> 30.2 us (0.984)
  Pallas kernels: 29.3 us -> 28.8 us
    pallas_call x1, Pallas kernels: 29.3 us -> 28.8 us  [local(): pl.pallas_call(kernel, out_shape=pltpu.VMEM((1, 1024), F32), in_specs=[hb...]
where the time goes in v8:
time: 30.2 us; the launch traced here: 30.1 us
  Pallas kernels  28.8 us (95%)
  between operations  0.67 us (2%)
  other arithmetic  0.62 us (2%)
    pallas_call x1, Pallas kernels, local(): pl.pallas_call(kernel, out_shape=pltpu.VMEM((1, 1024), F32), in_specs=[hb...  28.8 us
    mul x1, other arithmetic, local(): updated = conductivity * jnp.exp(-0.5 * jnp.tanh(gradient))  0.62 us

profile of v8, /device:TPU:1, one launch (start us, length us, event | category | flops | bytes accessed | tf_op | source)
XLA Modules:
  0.0 30.1 jit_solution(9659858176998035305)
XLA Ops:
  0.6 0.0 copy-start
  0.6 0.0 copy-start.1
  0.7 28.8 %shard_map.104 = f32[1,1024]{1,0:T(1,128)S(1)} custom-call(f32[2]{0:T(128)} %angular_hbm.1, f32[36,1,1024]{2,1,0:T(1,128)} %bitcast.5, f32[36,1,1024]{2,1,0:T(1,128)} %bitcast.6, f32[1,1,1024]{2,1,0:T(1,128)} %bitcast.8, s32[6,1,1024]{2,1,0:T(1,128)} %bitcast.7, s32[1,1,1024]{2,1,0:T(1,128)} %bitcast.9, f32[2,2,1,1280]{3,2,1,0:T(1,128)} %source_hbm.1, ...), custom_call_target="tpu_custom_call" | custom-call | tf_op jit(solution)/shard_map/pallas_call | solution.py:562
  29.5 0.0 copy-done
  29.5 0.0 copy-done.1
  29.5 0.6 %exponential_multiply_fusion = (f32[1,1024]{1,0:T(1,128)}, f32[1,1024]{1,0:T(1,128)}) fusion(f32[1,1024]{1,0:T(1,128)S(1)} %copy-done, s32[1,1024]{1,0:T(1,128)S(1)} %copy-done.1, f32[1,1024]{1,0:T(1,128)S(1)} %shard_map.104), kind=kLoop, calls=%fused_computation | loop fusion | flops 5120 | bytes 20480 | tf_op jit(solution)/shard_map/mul | solution.py:614
Async XLA Ops:
  0.6 28.9 %copy-start = (f32[1,1024]{1,0:T(1,128)S(1)}, f32[1,1024]{1,0:T(1,128)}, u32[]{:S(2)}) copy-start(f32[1,1024]{1,0:T(1,128)} %param.12) | copy-start | bytes 12292
  0.6 28.9 %copy-start.1 = (s32[1,1024]{1,0:T(1,128)S(1)}, s32[1,1024]{1,0:T(1,128)}, u32[]{:S(2)}) copy-start(s32[1,1024]{1,0:T(1,128)} %param.14) | copy-start | bytes 12292

commit v9 on v8

--- a/solution.py
+++ b/solution.py
@@ -14,7 +14,7 @@
 EDGES = 1280
 CHUNKS = EDGES // 128
 GROUPS = 4
-AHEAD = 2
+AHEAD = 3
 PARTS = 2
 STACK = 8 * PARTS
 HOPS = (0, 1, 2, 1)

time: 30.2 us -> 30.2 us (level)
  no operation moved by 1% of the time
where the time goes in v9:
time: 30.2 us; the launch traced here: 30.1 us
  Pallas kernels  28.8 us (95%)
  between operations  0.67 us (2%)
  other arithmetic  0.62 us (2%)
    pallas_call x1, Pallas kernels, local(): pl.pallas_call(kernel, out_shape=pltpu.VMEM((1, 1024), F32), in_specs=[hb...  28.8 us
    mul x1, other arithmetic, local(): updated = conductivity * jnp.exp(-0.5 * jnp.tanh(gradient))  0.62 us

profile of v9, /device:TPU:1, one launch (start us, length us, event | category | flops | bytes accessed | tf_op | source)
XLA Modules:
  0.0 30.1 jit_solution(15066215734057952633)
XLA Ops:
  0.6 0.0 copy-start
  0.6 0.0 copy-start.1
  0.7 28.8 %shard_map.104 = f32[1,1024]{1,0:T(1,128)S(1)} custom-call(f32[2]{0:T(128)} %angular_hbm.1, f32[36,1,1024]{2,1,0:T(1,128)} %bitcast.5, f32[36,1,1024]{2,1,0:T(1,128)} %bitcast.6, f32[1,1,1024]{2,1,0:T(1,128)} %bitcast.8, s32[6,1,1024]{2,1,0:T(1,128)} %bitcast.7, s32[1,1,1024]{2,1,0:T(1,128)} %bitcast.9, f32[2,2,1,1280]{3,2,1,0:T(1,128)} %source_hbm.1, ...), custom_call_target="tpu_custom_call" | custom-call | tf_op jit(solution)/shard_map/pallas_call | solution.py:562
  29.5 0.0 copy-done
  29.5 0.0 copy-done.1
  29.5 0.6 %exponential_multiply_fusion = (f32[1,1024]{1,0:T(1,128)}, f32[1,1024]{1,0:T(1,128)}) fusion(f32[1,1024]{1,0:T(1,128)S(1)} %copy-done, s32[1,1024]{1,0:T(1,128)S(1)} %copy-done.1, f32[1,1024]{1,0:T(1,128)S(1)} %shard_map.104), kind=kLoop, calls=%fused_computation | loop fusion | flops 5120 | bytes 20480 | tf_op jit(solution)/shard_map/mul | solution.py:614
Async XLA Ops:
  0.6 28.9 %copy-start = (f32[1,1024]{1,0:T(1,128)S(1)}, f32[1,1024]{1,0:T(1,128)}, u32[]{:S(2)}) copy-start(f32[1,1024]{1,0:T(1,128)} %param.12) | copy-start | bytes 12292
  0.6 28.9 %copy-start.1 = (s32[1,1024]{1,0:T(1,128)S(1)}, s32[1,1024]{1,0:T(1,128)}, u32[]{:S(2)}) copy-start(s32[1,1024]{1,0:T(1,128)} %param.14) | copy-start | bytes 12292
